TPU v7x, 32 devices: a whole 2x2x4 slice. The times are simulated.
32 devices in a mesh: branch: 2 (over core), frames: 16 (over z, y, x).
Axes of the slice: x: 2, y: 2, z: 4, core: 2. Of those that a mesh axis runs over, the one named last changes fastest.
Arguments:
- frames_in: bfloat16 [2, 16384, 384], P('branch', 'frames'), may hold values from -6 to 6
- seg_ids: int32 [2, 16384], P(None, 'frames'), may hold values from 0 to 63, as said below
- cotangent: bfloat16 [2, 16384, 384], P('branch', 'frames'), may hold values from -6 to 6
- params: float32 [2, 2363520], P('branch', 'frames')
- first_moment: float32 [2, 2363520], P('branch', 'frames')
- second_moment: float32 [2, 2363520], P('branch', 'frames'), as said below
Outputs:
- out_frames: bfloat16 [2, 16384, 384], P('branch', 'frames')
- input_grad: float32 [2, 16384, 384], P('branch', 'frames')
- clipped_grad: float32 [2, 2363520], P('branch', 'frames')
- vector_grad: float32 [2, 4224], P('branch', 'frames')
- grad_norm: float32 [], replicated
- first_new: float32 [2, 2363520], P('branch', 'frames')
- second_new: float32 [2, 2363520], P('branch', 'frames')
- new_params: float32 [2, 2363520], P('branch', 'frames')
Inputs may be any that keep to these rules, and one draw needn't show every extreme that they name: `seg_ids`: in each aligned block of 1024 frames of a branch (the same blocks in both branches) the segment numbers are whole segments, numbered without gaps, never decreasing, and starting at (block index) * 4; both branches' blocks hold the same numbers, 1 to 4 of them; the last block holds 4. `second_moment`: positive.
All inputs are finite; a program needn't handle non-finite values.
Results may differ from a plain program's by a relative error of at most 0.012.
Values may be sent and summed in bfloat16 or wider, within the bound.
A program may use at most 256 MiB of HBM per device.

v0:
```python
from functools import partial
import math

import jax
import jax.numpy as jnp
from jax import lax
from jax.sharding import PartitionSpec as P

HEADS = 8
HEAD_DIM = 48
D = 384
FF = 1536
NV = 11
STEP = 5


BETA_ONE = 0.9
BETA_TWO = 0.999
LEARN_RATE = 0.05
DECAY_RATE = 0.01
ADAM_EPS = 1e-08
NORM_EPS = 1e-05
MASKED = -1e30


def from_partner(array, axis, apart):
    return lax.ppermute(array, axis, [(i, i ^ 1 << apart) for i in range(lax.axis_size(axis))])


def layer_norm(values, gain, shift):
    centre = values - jnp.mean(values, -1, keepdims=True)
    spread = jnp.mean(centre * centre, -1, keepdims=True)
    return centre * lax.rsqrt(spread + NORM_EPS) * gain + shift


def unpack(flat, count):
    shapes = ((D, 3 * D), (D, D), (D, D), (D, 2 * D), (D, D), (D, FF), (FF, D), (NV, D))
    sliced = flat.reshape(count, flat.shape[0] // count)
    pieces = []
    offset = 0
    for rows_in, cols_out in shapes:
        width = rows_in * cols_out // count
        pieces.append(sliced[:, offset : offset + width].reshape(rows_in, cols_out))
        offset += width
    return pieces


def split_heads(tensor):
    return tensor.reshape(tensor.shape[0], HEADS, HEAD_DIM)


def matmul(left, right):
    return jnp.dot(left, right, preferred_element_type=jnp.float32)


def weight_grad(inputs, grads):
    return jnp.einsum("ri,rj->ij", inputs, grads, preferred_element_type=jnp.float32)


def back_input(grads, weight):
    return jnp.einsum("rj,ij->ri", grads, weight, preferred_element_type=jnp.float32)


def masked_scores(queries, keys_in, allowed, scale):
    scores = (
        jnp.einsum("qhe,khe->hqk", queries, keys_in, preferred_element_type=jnp.float32) * scale
    )
    return jnp.where(allowed[None], scores, MASKED)


def attend(queries, keys_in, values_in, allowed, scale):
    scores = masked_scores(queries, keys_in, allowed, scale)
    row_max = jnp.max(scores, -1, keepdims=True)
    raised = jnp.exp(scores - row_max)
    row_sum = jnp.sum(raised, -1, keepdims=True)
    weights = (raised / row_sum).astype(jnp.bfloat16)
    output = jnp.einsum("hqk,khe->qhe", weights, values_in, preferred_element_type=jnp.float32)
    return (output, row_max + jnp.log(row_sum))


def attend_back(queries, keys_in, values_in, allowed, scale, log_sum, grad_out):
    probs = jnp.exp(masked_scores(queries, keys_in, allowed, scale) - log_sum)
    grad_probs = jnp.einsum("qhe,khe->hqk", grad_out, values_in, preferred_element_type=jnp.float32)
    grad_values = jnp.einsum(
        "hqk,qhe->khe", probs.astype(jnp.bfloat16), grad_out, preferred_element_type=jnp.float32
    )
    centred = grad_probs - jnp.sum(probs * grad_probs, -1, keepdims=True)
    grad_scores = (probs * centred).astype(jnp.bfloat16)
    grad_queries = (
        jnp.einsum("hqk,khe->qhe", grad_scores, keys_in, preferred_element_type=jnp.float32) * scale
    )
    grad_keys = (
        jnp.einsum("hqk,qhe->khe", grad_scores, queries, preferred_element_type=jnp.float32) * scale
    )
    return (
        grad_queries.astype(jnp.bfloat16),
        grad_keys.astype(jnp.bfloat16),
        grad_values.astype(jnp.bfloat16),
    )


def on_device(frames_in, seg_ids, cotangent, params, first_moment, second_moment):
    frames = frames_in[0].astype(jnp.float32)
    rows = frames.shape[0]
    count = lax.axis_size("frames")
    side = lax.axis_index("branch")
    own_seg = jnp.where(side == 0, seg_ids[0], seg_ids[1])
    far_seg = jnp.where(side == 0, seg_ids[1], seg_ids[0])
    self_mask = own_seg[:, None] == own_seg[None, :]
    cross_mask = own_seg[:, None] == far_seg[None, :]
    scale = 1.0 / math.sqrt(HEAD_DIM)
    shard16 = params.astype(jnp.bfloat16)
    whole = lax.all_gather(shard16, "frames", axis=1, tiled=True)[0]
    w_qkv, w_self, w_query, w_keyval, w_cross, w_up, w_down, vec16 = unpack(whole, count)
    vectors = vec16.astype(jnp.float32)
    normed, norm1_back = jax.vjp(layer_norm, frames, vectors[0], vectors[1])
    normed16 = normed.astype(jnp.bfloat16)
    joined16 = matmul(normed16, w_qkv).astype(jnp.bfloat16)
    query16 = split_heads(joined16[:, :D])
    key16 = split_heads(joined16[:, D : 2 * D])
    value16 = split_heads(joined16[:, 2 * D :])
    attended, self_lse = attend(query16, key16, value16, self_mask, scale)
    attended16 = attended.reshape(rows, D).astype(jnp.bfloat16)
    self_out = matmul(attended16, w_self)
    hidden = frames + vectors[8] * self_out
    cross_in, norm2_back = jax.vjp(layer_norm, hidden, vectors[2], vectors[3])
    cross_in16 = cross_in.astype(jnp.bfloat16)
    cross_q16 = matmul(cross_in16, w_query).astype(jnp.bfloat16)
    source, norm3_back = jax.vjp(layer_norm, hidden, vectors[4], vectors[5])
    source16 = source.astype(jnp.bfloat16)
    keyval16 = matmul(source16, w_keyval).astype(jnp.bfloat16)
    far_kv = from_partner(keyval16, "branch", 0)
    far_keys = split_heads(far_kv[:, :D])
    far_values = split_heads(far_kv[:, D:])
    cross_heads = split_heads(cross_q16)
    mixed, cross_lse = attend(cross_heads, far_keys, far_values, cross_mask, scale)
    mixed16 = mixed.reshape(rows, D).astype(jnp.bfloat16)
    cross_out = matmul(mixed16, w_cross)
    second_h = hidden + vectors[9] * cross_out
    ffn_in, norm4_back = jax.vjp(layer_norm, second_h, vectors[6], vectors[7])
    ffn_in16 = ffn_in.astype(jnp.bfloat16)
    pre_act = matmul(ffn_in16, w_up)
    activated, gelu_back = jax.vjp(partial(jax.nn.gelu, approximate=False), pre_act)
    activated16 = activated.astype(jnp.bfloat16)
    ffn_out = matmul(activated16, w_down)
    result = second_h + vectors[10] * ffn_out
    grad_out = cotangent[0].astype(jnp.float32)
    grad_ls3 = jnp.sum(grad_out * ffn_out, 0)
    grad_ffn16 = (grad_out * vectors[10]).astype(jnp.bfloat16)
    grad_down = weight_grad(activated16, grad_ffn16)
    grad_act = back_input(grad_ffn16, w_down)
    grad_pre16 = gelu_back(grad_act)[0].astype(jnp.bfloat16)
    grad_up = weight_grad(ffn_in16, grad_pre16)
    grad_h2_ln, grad_g4, grad_c4 = norm4_back(back_input(grad_pre16, w_up))
    grad_h2 = grad_out + grad_h2_ln
    grad_ls2 = jnp.sum(grad_h2 * cross_out, 0)
    grad_cross16 = (grad_h2 * vectors[9]).astype(jnp.bfloat16)
    grad_wcross = weight_grad(mixed16, grad_cross16)
    grad_mixed16 = back_input(grad_cross16, w_cross).astype(jnp.bfloat16)
    grad_cq16, grad_far_keys, grad_far_values = attend_back(
        cross_heads, far_keys, far_values, cross_mask, scale, cross_lse, split_heads(grad_mixed16)
    )
    returned = jnp.concatenate(
        [grad_far_keys.reshape(rows, D), grad_far_values.reshape(rows, D)], 1
    )
    grad_keyval16 = from_partner(returned, "branch", 0)
    grad_wkeyval = weight_grad(source16, grad_keyval16)
    grad_h_kv, grad_g3, grad_c3 = norm3_back(back_input(grad_keyval16, w_keyval))
    grad_cq_flat = grad_cq16.reshape(rows, D)
    grad_wquery = weight_grad(cross_in16, grad_cq_flat)
    grad_h_q, grad_g2, grad_c2 = norm2_back(back_input(grad_cq_flat, w_query))
    grad_hidden = grad_h2 + grad_h_q + grad_h_kv
    grad_ls1 = jnp.sum(grad_hidden * self_out, 0)
    grad_self16 = (grad_hidden * vectors[8]).astype(jnp.bfloat16)
    grad_wself = weight_grad(attended16, grad_self16)
    grad_att16 = back_input(grad_self16, w_self).astype(jnp.bfloat16)
    grad_q16, grad_k16, grad_v16 = attend_back(
        query16, key16, value16, self_mask, scale, self_lse, split_heads(grad_att16)
    )
    grad_joined16 = jnp.concatenate(
        [grad_q16.reshape(rows, D), grad_k16.reshape(rows, D), grad_v16.reshape(rows, D)], 1
    )
    grad_wqkv = weight_grad(normed16, grad_joined16)
    grad_x_ln, grad_g1, grad_c1 = norm1_back(back_input(grad_joined16, w_qkv))
    input_grad = grad_hidden + grad_x_ln
    grad_vectors = jnp.stack(
        [
            grad_g1,
            grad_c1,
            grad_g2,
            grad_c2,
            grad_g3,
            grad_c3,
            grad_g4,
            grad_c4,
            grad_ls1,
            grad_ls2,
            grad_ls3,
        ]
    )
    pieces = [
        grad_wqkv,
        grad_wself,
        grad_wquery,
        grad_wkeyval,
        grad_wcross,
        grad_up,
        grad_down,
        grad_vectors,
    ]
    flat_grad = jnp.concatenate([piece.reshape(count, -1) for piece in pieces], 1).reshape(1, -1)
    reduced = lax.psum_scatter(flat_grad, "frames", scatter_dimension=1, tiled=True)
    local_square = jnp.sum(reduced * reduced)
    square_sum = lax.psum(local_square, ("branch", "frames"))
    grad_norm = jnp.sqrt(square_sum)
    total_params = params.shape[1] * count
    total_rows = rows * count
    threshold = 0.01 * math.sqrt(2.0 * total_params * total_rows)
    clipped = reduced * jnp.minimum(1.0, threshold / grad_norm)
    vec_width = NV * D // count
    vector_grad = clipped[:, clipped.shape[1] - vec_width :]
    first_new = BETA_ONE * first_moment + (1.0 - BETA_ONE) * clipped
    second_new = BETA_TWO * second_moment + (1.0 - BETA_TWO) * clipped * clipped
    mean_hat = first_new / (1.0 - BETA_ONE**STEP)
    square_hat = second_new / (1.0 - BETA_TWO**STEP)
    new_params = params - LEARN_RATE * (
        mean_hat / (jnp.sqrt(square_hat) + ADAM_EPS) + DECAY_RATE * params
    )
    return (
        result.astype(jnp.bfloat16)[None],
        input_grad[None],
        clipped,
        vector_grad,
        grad_norm,
        first_new,
        second_new,
        new_params,
    )


def solution(mesh):
    placed = (
        P("branch", "frames", None),
        P(None, "frames"),
        P("branch", "frames", None),
        P("branch", "frames"),
        P("branch", "frames"),
        P("branch", "frames"),
    )
    return jax.shard_map(
        on_device,
        mesh=mesh,
        in_specs=placed,
        out_specs=(
            P("branch", "frames", None),
            P("branch", "frames", None),
            P("branch", "frames"),
            P("branch", "frames"),
            P(),
            P("branch", "frames"),
            P("branch", "frames"),
            P("branch", "frames"),
        ),
        check_vma=False,
    )
```

profile of v0, /device:TPU:0, one launch (start us, length us, event | category | flops | bytes accessed | tf_op | source)
XLA Modules:
  0.0 1035.3 jit_solution(14357924247843391103)
XLA Ops:
  7.2 6.7 convert_reduce_fusion.1
  15.9 2.6 broadcast.219
  18.5 5.8 dynamic-update-slice
  27.9 2.3 broadcast_compare_fusion
  30.2 177.6 %all-reduce.5.cloned.1.call-done = bf16[2363520]{0:T(1024)(128)(2,1)} async-done(((bf16[2363520]{0:T(1024)(128)(2,1)}), bf16[2363520]{0:T(1024)(128)(2,1)}) %all-reduce.5.cloned.1.call-update) | async-done | bytes 4727056
  207.8 10.9 %reshape_squeeze.3 = bf16[16,147720]{1,0:T(8,128)(2,1)} reshape(bf16[2363520]{0:T(1024)(128)(2,1)} %all-reduce.5.cloned.1.call-done) | data formatting | bytes 9454080 | tf_op jit(solution)/shard_map/reshape;squeeze | solution.py:38
  219.5 2.1 fusion.89
  228.0 1.7 copy.76
  232.1 27.1 %fusion.93 = (f32[8,1024]{1,0:T(8,128)S(1)}, f32[8,1024,1024]{1,2,0:T(8,128)}) fusion(bf16[1024,8,48]{0,2,1:T(8,128)(2,1)S(1)} %bitcast.156, bf16[1024,8,48]{0,2,1:T(8,128)(2,1)S(1)} %bitcast.158, pred[1024,1024]{0,1:T(8,128)(4,1)} %get-tuple-element.89), kind=kOutput, calls=%fused_computation.189 | convolution fusion | flops 830464000 | bytes 36208640 | tf_op jit(solution)/shard_map/qhe,khe->hqk/dot_general | solution.py:66
  259.2 13.8 %fusion = f32[8,1024]{1,0:T(8,128)S(1)} fusion(f32[8,1024,1024]{1,2,0:T(8,128)} %get-tuple-element.93, f32[8,1024]{1,0:T(8,128)S(1)} %get-tuple-element.92), kind=kLoop, calls=%fused_computation.12 | loop fusion | flops 16769024 | bytes 33619968 | tf_op jit(solution)/shard_map/reduce_sum | solution.py:75
  273.1 13.6 %fusion.48 = bf16[8,48,1024]{2,1,0:T(8,128)(2,1)S(1)} fusion(bf16[1024,8,48]{0,2,1:T(8,128)(2,1)S(1)} %bitcast.170, f32[8,1024,1024]{1,2,0:T(8,128)} %get-tuple-element.93, f32[8,1024]{1,0:T(8,128)S(1)} %fusion, f32[8,1024]{1,0:T(8,128)S(1)} %get-tuple-element.92), kind=kOutput, calls=%fused_computation.106 | convolution fusion | flops 830865408 | bytes 35192832 | tf_op jit(solution)/shard_map/hqk,khe->qhe/dot_general | solution.py:77
  286.8 1.8 fusion.86
  289.6 2.3 convolution_convert_fusion.1
  294.5 2.4 reshape.376
  299.9 2.7 fusion.91
  305.2 15.2 %fusion.94 = (f32[8,1024]{1,0:T(8,128)S(1)}, f32[8,1024,1024]{1,2,0:T(8,128)}) fusion(bf16[1024,8,48]{0,2,1:T(8,128)(2,1)S(1)} %bitcast.160, bf16[1024,8,48]{0,2,1:T(8,128)(2,1)S(1)} %bitcast.162, pred[1024,1024]{0,1:T(8,128)(4,1)} %get-tuple-element.88), kind=kOutput, calls=%fused_computation.190 | convolution fusion | flops 830464000 | bytes 36208640 | tf_op jit(solution)/shard_map/qhe,khe->hqk/dot_general | solution.py:66
  320.4 13.1 %fusion.1 = f32[8,1024]{1,0:T(8,128)S(1)} fusion(f32[8,1024,1024]{1,2,0:T(8,128)} %get-tuple-element.96, f32[8,1024]{1,0:T(8,128)S(1)} %get-tuple-element.95), kind=kLoop, calls=%fused_computation.13 | loop fusion | flops 16769024 | bytes 33619968 | tf_op jit(solution)/shard_map/reduce_sum | solution.py:75
  333.5 14.0 %fusion.47 = bf16[8,48,1024]{2,1,0:T(8,128)(2,1)S(1)} fusion(bf16[1024,8,48]{0,2,1:T(8,128)(2,1)S(1)} %bitcast.173, f32[8,1024,1024]{1,2,0:T(8,128)} %get-tuple-element.96, f32[8,1024]{1,0:T(8,128)S(1)} %fusion.1, f32[8,1024]{1,0:T(8,128)S(1)} %get-tuple-element.95), kind=kOutput, calls=%fused_computation.105 | convolution fusion | flops 830865408 | bytes 35192832 | tf_op jit(solution)/shard_map/hqk,khe->qhe/dot_general | solution.py:77
  347.6 1.8 fusion.85
  350.7 16.7 %multiply_convert_fusion.2 = (bf16[1024,1536]{1,0:T(8,128)(2,1)}, f32[1024,1536]{1,0:T(8,128)S(1)}, f32[1024,1536]{1,0:T(8,128)S(1)}) fusion(bf16[384,1536]{1,0:T(8,128)(2,1)S(1)} %copy-done.45, f32[1024,384]{0,1:T(8,128)S(1)} %get-tuple-element.68, f32[384]{0:T(512)S(1)} %copy-done.99, f32[384]{0:T(512)S(1)} %copy-done.82, f32[1024]{0:T(1024)S(1)} %fusion.73, ...), kind=kOutput, calls=%fused_computation.25 | convolution fusion | flops 1312161792 | bytes 18492416 | tf_op jit(solution)/shard_map/dot_general | solution.py:53
  367.3 3.8 add_convert_fusion
  371.1 3.0 fusion.98
  374.1 3.1 copy.83
  377.2 2.0 multiply_reduce_fusion.4
  382.2 14.4 %fusion.41 = bf16[8,48,1024]{2,1,0:T(8,128)(2,1)} fusion(bf16[1024,8,48]{0,2,1:T(8,128)(2,1)} %bitcast.164, f32[8,1024,1024]{1,2,0:T(8,128)} %get-tuple-element.96, f32[8,1024]{1,0:T(8,128)S(1)} %log_add_fusion.1), kind=kOutput, calls=%fused_computation.100 | convolution fusion | flops 822476800 | bytes 35160064 | tf_op jit(solution)/shard_map/hqk,qhe->khe/dot_general | solution.py:84
  396.6 22.8 %multiply_reduce_fusion.1 = (f32[8,1024]{1,0:T(8,128)S(1)}, f32[8,1024,1024]{1,2,0:T(8,128)}) fusion(f32[8,1024,1024]{1,2,0:T(8,128)} %get-tuple-element.96, f32[8,1024]{1,0:T(8,128)S(1)} %log_add_fusion.1, bf16[1024,8,48]{0,2,1:T(8,128)(2,1)} %bitcast.165, bf16[1024,8,48]{0,2,1:T(8,128)(2,1)} %bitcast.172), kind=kOutput, calls=%fused_computation.4 | convolution fusion | flops 830464000 | bytes 68747264 | tf_op jit(solution)/shard_map/qhe,khe->hqk/dot_general | solution.py:83
  419.3 28.1 %multiply_convert_fusion.1 = bf16[8,1024,1024]{1,2,0:T(8,128)(2,1)} fusion(f32[8,1024,1024]{1,2,0:T(8,128)} %get-tuple-element.100, f32[8,1024,1024]{1,2,0:T(8,128)} %get-tuple-element.96, f32[8,1024]{1,0:T(8,128)S(1)} %get-tuple-element.99, f32[8,1024]{1,0:T(8,128)S(1)} %log_add_fusion.1), kind=kLoop, calls=%fused_computation.3 | loop fusion | flops 33554432 | bytes 83951616 | tf_op jit(solution)/shard_map/convert_element_type | solution.py:88
  447.5 12.1 %multiply_convert_fusion.6 = bf16[8,48,1024]{2,1,0:T(8,128)(2,1)} fusion(bf16[1024,8,48]{0,2,1:T(8,128)(2,1)} %bitcast.161, bf16[8,1024,1024]{1,2,0:T(8,128)(2,1)} %multiply_convert_fusion.1), kind=kOutput, calls=%fused_computation.88 | convolution fusion | flops 806092800 | bytes 18350080 | tf_op jit(solution)/shard_map/hqk,qhe->khe/dot_general | solution.py:93
  459.5 9.1 multiply_convert_fusion.7
  470.5 2.0 fusion.96
  472.5 3.1 copy.85
  475.5 2.8 fusion.99
  478.3 2.0 reshape.388
  480.3 2.8 fusion.100
  483.1 2.0 reshape.390
  485.0 4.8 fusion.79
  489.9 3.1 reshape.391
  492.9 5.4 fusion.56
  498.4 2.9 reshape.392
  503.0 4.3 fusion.97
  507.3 3.1 copy.88
  510.4 2.5 multiply_reduce_fusion.8
  513.2 1.7 multiply_reduce_fusion.5
  515.5 6.5 fusion.33
  523.7 14.3 %fusion.44 = bf16[8,48,1024]{2,1,0:T(8,128)(2,1)} fusion(bf16[1024,8,48]{0,2,1:T(8,128)(2,1)S(1)} %bitcast.166, f32[8,1024,1024]{1,2,0:T(8,128)} %get-tuple-element.93, f32[8,1024]{1,0:T(8,128)S(1)} %copy-done.44), kind=kOutput, calls=%fused_computation.101 | convolution fusion | flops 822476800 | bytes 35160064 | tf_op jit(solution)/shard_map/hqk,qhe->khe/dot_general | solution.py:84
  538.0 21.9 %multiply_reduce_fusion = (f32[8,1024]{1,0:T(8,128)S(1)}, f32[8,1024,1024]{1,2,0:T(8,128)}) fusion(f32[8,1024,1024]{1,2,0:T(8,128)} %get-tuple-element.93, f32[8,1024]{1,0:T(8,128)S(1)} %copy-done.44, bf16[1024,8,48]{0,2,1:T(8,128)(2,1)S(1)} %bitcast.167, bf16[1024,8,48]{0,2,1:T(8,128)(2,1)S(1)} %bitcast.171), kind=kOutput, calls=%fused_computation.1 | convolution fusion | flops 830464000 | bytes 68747264 | tf_op jit(solution)/shard_map/qhe,khe->hqk/dot_general | solution.py:83
  559.9 28.6 %multiply_convert_fusion = bf16[8,1024,1024]{1,2,0:T(8,128)(2,1)} fusion(f32[8,1024,1024]{1,2,0:T(8,128)} %get-tuple-element.102, f32[8,1024,1024]{1,2,0:T(8,128)} %get-tuple-element.93, f32[8,1024]{1,0:T(8,128)S(1)} %get-tuple-element.101, f32[8,1024]{1,0:T(8,128)S(1)} %copy-done.44), kind=kLoop, calls=%fused_computation | loop fusion | flops 33554432 | bytes 83951616 | tf_op jit(solution)/shard_map/convert_element_type | solution.py:88
  588.5 11.9 %multiply_convert_fusion.3 = bf16[8,48,1024]{2,1,0:T(8,128)(2,1)} fusion(bf16[1024,8,48]{0,2,1:T(8,128)(2,1)S(1)} %bitcast.157, bf16[8,1024,1024]{1,2,0:T(8,128)(2,1)} %multiply_convert_fusion), kind=kOutput, calls=%fused_computation.83 | convolution fusion | flops 806092800 | bytes 18350080 | tf_op jit(solution)/shard_map/hqk,qhe->khe/dot_general | solution.py:93
  600.4 8.9 multiply_convert_fusion.4
  609.5 3.2 fusion.95
  612.8 2.6 fusion.49
  616.0 3.1 copy.92
  619.1 1.8 fusion.36
  622.3 2.9 reshape.386
  625.2 2.8 constant_dynamic-update-slice_fusion.7
  628.1 3.3 fusion.81
  642.3 13.0 %reshape.426 = f32[2363520]{0:T(1024)} reshape(f32[16,147720]{1,0:T(8,128)} %constant_dynamic-update-slice_fusion) | data formatting | bytes 18908160
  655.3 36.7 %reshape.402 = f32[1,2363520]{1,0:T(1,128)} reshape(f32[2363520]{0:T(1024)} %reshape.426) | data formatting | bytes 18908160 | tf_op jit(solution)/shard_map/reshape | solution.py:211
  694.3 3.1 add_bitcast_fusion
  697.4 276.3 %all-reduce.7.cloned.1.call-done = f32[1,2363520]{1,0:T(1,128)} async-done(((f32[1,2363520]{1,0:T(1,128)}), f32[1,2363520]{1,0:T(1,128)}) %all-reduce.7.cloned.1.call-update) | async-done | bytes 9454096
  973.7 2.9 multiply_reduce_fusion.12
  976.7 3.2 copy.99
  979.8 39.8 %psum.7 = f32[]{:T(128)} all-reduce(f32[]{:T(128)} %multiply_reduce_fusion.12), channel_id=1, replica_groups=mesh['branch'=2,'frames'=16] {'branch','frames'}, use_global_device_ids=true, to_apply=%region_33.34 | all-reduce | flops 1 | bytes 8 | tf_op jit(solution)/shard_map/psum | solution.py:214
  1020.3 6.0 multiply_subtract_fusion
  (294 shorter events, 49.0 us)
Async XLA Ops:
  7.2 200.7 %all-reduce.5.cloned.1.call-start = ((), (), s32[]{:S(2)}) async-start(), calls=%async_computation | async-start | bytes 9457664
  24.3 2.3 copy-start.50
  24.4 949.3 %all-reduce.7.cloned.1.call-start = ((), (), s32[]{:S(2)}) async-start(), calls=%async_computation.1 | async-start | bytes 18908160
  26.9 259.8 %copy-start = (bf16[1,1024,384]{1,2,0:T(8,128)(2,1)}, bf16[1,1024,384]{1,2,0:T(8,128)(2,1)S(1)}, u32[]{:S(2)}) copy-start(bf16[1,1024,384]{1,2,0:T(8,128)(2,1)S(1)} %copy.73) | copy-start | bytes 2359300
  27.1 195.7 %copy-start.62 = (f32[1024]{0:T(1024)}, f32[1024]{0:T(1024)S(1)}, u32[]{:S(2)}) copy-start(f32[1024]{0:T(1024)S(1)} %broadcast_multiply_fusion.2) | copy-start | bytes 12292
  27.9 194.8 %copy-start.68 = (f32[1024]{0:T(1024)}, f32[1024]{0:T(1024)S(1)}, u32[]{:S(2)}) copy-start(f32[1024]{0:T(1024)S(1)} %fusion.71) | copy-start | bytes 12292
  219.5 2.8 slice-start.2
  222.3 64.4 %copy-start.80 = (f32[384]{0:T(512)}, f32[384]{0:T(512)S(1)}, u32[]{:S(2)}) copy-start(f32[384]{0:T(512)S(1)} %get-tuple-element.56) | copy-start | bytes 4612
  222.3 66.5 %copy-start.78 = (f32[384]{0:T(512)}, f32[384]{0:T(512)S(1)}, u32[]{:S(2)}) copy-start(f32[384]{0:T(512)S(1)} %get-tuple-element.52) | copy-start | bytes 4612
  222.3 76.7 %copy-start.66 = (f32[384]{0:T(512)}, f32[384]{0:T(512)S(1)}, u32[]{:S(2)}) copy-start(f32[384]{0:T(512)S(1)} %get-tuple-element.50) | copy-start | bytes 4612
  227.7 3.3 slice-start.3
  228.0 4.1 copy-start.11
  229.7 29.5 %copy-start.13 = (bf16[1024,384]{0,1:T(8,128)(2,1)}, bf16[1024,384]{0,1:T(8,128)(2,1)S(1)}, u32[]{:S(2)}) copy-start(bf16[1024,384]{0,1:T(8,128)(2,1)S(1)} %copy.76) | copy-start | bytes 2359300
  231.0 55.7 %copy-start.39 = (bf16[384,384]{1,0:T(8,128)(2,1)}, bf16[384,384]{1,0:T(8,128)(2,1)S(1)}, u32[]{:S(2)}) copy-start(bf16[384,384]{1,0:T(8,128)(2,1)S(1)} %reshape.369) | copy-start | bytes 884740
  259.2 13.9 %copy-start.56 = (f32[8,1024]{1,0:T(8,128)}, f32[8,1024]{1,0:T(8,128)S(1)}, u32[]{:S(2)}) copy-start(f32[8,1024]{1,0:T(8,128)S(1)} %get-tuple-element.92) | copy-start | bytes 98308
  259.2 13.9 %copy-start.28 = (bf16[1024,384]{0,1:T(8,128)(2,1)S(1)}, bf16[1024,384]{0,1:T(8,128)(2,1)}, u32[]{:S(2)}) copy-start(bf16[1024,384]{0,1:T(8,128)(2,1)} %copy.74) | copy-start | bytes 2359300
  259.2 32.7 %slice-start = ((s8[4730880]{0:T(1024)(128)(4,1)}), s8[4194304]{0:T(1024)(128)(4,1)S(1)}, s32[]{:S(2)}) async-start(s8[4730880]{0:T(1024)(128)(4,1)} %bitcast.154), calls=%async_computation.2 | async-start | bytes 8388608
  273.0 13.7 %copy-start.60 = (f32[8,1024]{1,0:T(8,128)}, f32[8,1024]{1,0:T(8,128)S(1)}, u32[]{:S(2)}) copy-start(f32[8,1024]{1,0:T(8,128)S(1)} %fusion) | copy-start | bytes 98308
  273.1 18.9 %slice-start.1 = ((s8[4730880]{0:T(1024)(128)(4,1)}), s8[536576]{0:T(1024)(128)(4,1)S(1)}, s32[]{:S(2)}) async-start(s8[4730880]{0:T(1024)(128)(4,1)} %bitcast.154), calls=%async_computation.3 | async-start | bytes 1073152
  288.6 10.4 %copy-start.58 = (f32[1024]{0:T(1024)}, f32[1024]{0:T(1024)S(1)}, u32[]{:S(2)}) copy-start(f32[1024]{0:T(1024)S(1)} %broadcast_multiply_fusion.1) | copy-start | bytes 12292
  288.8 3.1 copy-start.73
  288.8 10.2 copy-start.64
  291.9 8.0 collective-permute-start
  293.3 6.0 copy-start.37
  299.3 3.3 copy-start.23
  299.9 5.3 copy-start.15
  305.2 15.2 %copy-start.16 = (bf16[1024,384]{0,1:T(8,128)(2,1)}, bf16[1024,384]{0,1:T(8,128)(2,1)S(1)}, u32[]{:S(2)}) copy-start(bf16[1024,384]{0,1:T(8,128)(2,1)S(1)} %copy.79) | copy-start | bytes 2359300
  320.4 13.1 %copy-start.30 = (bf16[1024,384]{0,1:T(8,128)(2,1)S(1)}, bf16[1024,384]{0,1:T(8,128)(2,1)}, u32[]{:S(2)}) copy-start(bf16[1024,384]{0,1:T(8,128)(2,1)} %copy.78) | copy-start | bytes 2359300
  333.5 14.1 %copy-start.83 = (f32[384]{0:T(512)S(1)}, f32[384]{0:T(512)}, u32[]{:S(2)}) copy-start(f32[384]{0:T(512)} %get-tuple-element.53) | copy-start | bytes 4612
  350.6 16.7 %copy-start.19 = (bf16[1,1024,384]{1,2,0:T(8,128)(2,1)S(1)}, bf16[1,1024,384]{1,2,0:T(8,128)(2,1)}, u32[]{:S(2)}) copy-start(bf16[1,1024,384]{1,2,0:T(8,128)(2,1)} %copy.82) | copy-start | bytes 2359300
  350.6 16.7 %copy-start.27 = (bf16[1536,384]{1,0:T(8,128)(2,1)S(1)}, bf16[1536,384]{1,0:T(8,128)(2,1)}, u32[]{:S(2)}) copy-start(bf16[1536,384]{1,0:T(8,128)(2,1)} %reshape.377) | copy-start | bytes 3538948
  350.6 16.7 %copy-start.85 = (f32[384]{0:T(512)S(1)}, f32[384]{0:T(512)}, u32[]{:S(2)}) copy-start(f32[384]{0:T(512)} %get-tuple-element.46) | copy-start | bytes 4612
  371.1 3.0 copy-start.102
  459.5 9.2 copy-start.32
  459.5 9.2 copy-start.36
  470.0 33.0 %collective-permute-start.1 = (bf16[1024,768]{0,1:T(8,128)(2,1)}, bf16[1024,768]{0,1:T(8,128)(2,1)}, u32[]{:S(2)}, u32[]{:S(2)}) collective-permute-start(bf16[1024,768]{0,1:T(8,128)(2,1)} %pad_maximum_fusion.1), channel_id=1, source_target_pairs={{0,16},{16,0},{1,17},{17,1},{2,18},{18,2},{3,19},{19,3},{4,20},{20... | collective-permute-start | bytes 4718600 | tf_op jit(solution)/shard_map/ppermute | solution.py:27
  507.3 3.1 copy-start.59
  507.3 3.1 copy-start.67
  507.3 3.1 copy-start.79
  510.4 2.5 copy-start.74
  510.4 2.5 copy-start.5
  510.4 2.8 copy-start.6
  510.4 2.8 copy-start.65
  510.4 4.6 copy-start.26
  515.5 7.6 copy-start.40
  515.5 7.6 copy-start.81
  523.7 14.3 %copy-start.29 = (bf16[1024,384]{0,1:T(8,128)(2,1)S(1)}, bf16[1024,384]{0,1:T(8,128)(2,1)}, u32[]{:S(2)}) copy-start(bf16[1024,384]{0,1:T(8,128)(2,1)} %copy.74) | copy-start | bytes 2359300
  559.9 28.6 %copy-start.12 = (bf16[1024,384]{0,1:T(8,128)(2,1)S(1)}, bf16[1024,384]{0,1:T(8,128)(2,1)}, u32[]{:S(2)}) copy-start(bf16[1024,384]{0,1:T(8,128)(2,1)} %copy-done.11) | copy-start | bytes 2359300
  588.5 11.9 %copy-start.14 = (bf16[1024,384]{0,1:T(8,128)(2,1)S(1)}, bf16[1024,384]{0,1:T(8,128)(2,1)}, u32[]{:S(2)}) copy-start(bf16[1024,384]{0,1:T(8,128)(2,1)} %copy-done.13) | copy-start | bytes 2359300
  600.4 9.0 copy-start.47
  600.4 9.0 copy-start.48
  600.4 9.0 copy-start.51
  609.4 3.3 copy-start.1
  609.4 3.3 copy-start.63
  609.4 3.3 copy-start.69
  609.4 3.3 copy-start.76
  609.5 3.3 copy-start.98
  612.7 2.6 copy-start.3
  612.7 2.6 copy-start.35
  631.5 2.8 copy-start.43
  637.5 2.5 copy-start.18
  976.6 43.7 %copy-start.41 = (f32[1,147720]{1,0:T(1,128)S(1)}, f32[1,147720]{1,0:T(1,128)}, u32[]{:S(2)}) copy-start(f32[1,147720]{1,0:T(1,128)} %param.9) | copy-start | bytes 1772644
  976.6 43.7 %copy-start.53 = (f32[1,147720]{1,0:T(1,128)S(1)}, f32[1,147720]{1,0:T(1,128)}, u32[]{:S(2)}) copy-start(f32[1,147720]{1,0:T(1,128)} %param.11) | copy-start | bytes 1772644
  976.6 43.7 %copy-start.54 = (f32[1,147720]{1,0:T(1,128)S(1)}, f32[1,147720]{1,0:T(1,128)}, u32[]{:S(2)}) copy-start(f32[1,147720]{1,0:T(1,128)} %param.10) | copy-start | bytes 1772644
  (47 other events, 73.1 us)
Sparse Core Ops, SparseCore 0:
  24.5 183.3 all-reduce.4
  692.1 281.5 all-reduce.6
where the time goes:
time: 1040 us
  waiting for transfers between devices  454 us (44%)
  matrix products  257 us (25%)
  local copies, waits for them, and re-layouts  146 us (14%)
  other arithmetic  118 us (11%)
  blocking collectives  39.8 us (4%)
  between operations  18.8 us (2%)
    unnamed x4, waiting for transfers between devices  454 us
    convert_element_type x2, other arithmetic, attend_back(): grad_scores = (probs * centred).astype(jnp.bfloat16)  56.7 us
    unnamed x225, local copies, waits for them, and re-layouts  47.2 us
    dot_general x2, matrix products, attend_back(): jnp.einsum('qhe,khe->hqk', grad_out, values_in, preferred_element_type=jn...  44.7 us
    dot_general x2, matrix products, masked_scores(): jnp.einsum('qhe,khe->hqk', queries, keys_in, preferred_element_type=jnp.f...  42.2 us
    psum x1, blocking collectives, on_device(): square_sum = lax.psum(local_square, ('branch', 'frames'))  39.8 us
    reshape x1, local copies, waits for them, and re-layouts, on_device(): jnp.concatenate([piece.reshape(count, -1) for piece in pieces], 1)  36.7 us
    dot_general x7, matrix products, matmul(): return jnp.dot(left, right, preferred_element_type=jnp.float32)  31.3 us
  transfers between devices with their start and end apart: 4, of which 2 were waited for; matrix products, arithmetic and copies ran while one was open for 5% of the time, Pallas kernels for 0%

commit v1 on v0

--- a/solution.py
+++ b/solution.py
@@ -4,6 +4,8 @@
 import jax
 import jax.numpy as jnp
 from jax import lax
+from jax.experimental import pallas as pl
+from jax.experimental.pallas import tpu as pltpu
 from jax.sharding import PartitionSpec as P
 
 HEADS = 8
@@ -238,6 +240,589 @@
     )
 
 
+MESH = pl.DeviceIdType.MESH
+BF = jnp.bfloat16
+F32 = jnp.float32
+C2 = math.log2(math.e) / math.sqrt(HEAD_DIM)
+SCALE = 1.0 / math.sqrt(HEAD_DIM)
+N = 1024
+TILE = 256
+LEAD = 16
+DOWN = LEAD + 36 * 24
+ROWS = DOWN + 288
+FLAT = 1160
+QKV, SELF, QUERY, KEYVAL, CROSS, UP = (0, 9), (216, 3), (288, 3), (360, 6), (504, 3), (576, 12)
+OUT_ORDER = [(m, c) for m in (QKV, SELF, QUERY, KEYVAL, CROSS, UP) for c in range(m[1])]
+BACK_ORDER = [e for s in range(3) for e in ((QKV, s), (QKV, 3 + s), (QKV, 6 + s), (SELF, s))] + OUT_ORDER[12:]
+OUT_PIECES = ((0, 112), (112, 96), (208, 48), (256, 336), (592, 288), (880, 288))
+BACK_PIECES = ((880, 288), (592, 288), (304, 288), (16, 96), (112, 96), (208, 96))
+
+
+def remote(src, dst, send, recv, **device):
+    return pltpu.make_async_remote_copy(
+        src_ref=src, dst_ref=dst, send_sem=send, recv_sem=recv, device_id=device, device_id_type=MESH
+    )
+
+
+def mm(a, b):
+    return lax.dot_general(a, b, (((1,), (0,)), ((), ())), preferred_element_type=F32)
+
+
+def mm_nt(a, b):
+    return lax.dot_general(a, b, (((1,), (1,)), ((), ())), preferred_element_type=F32)
+
+
+def loop(start, stop, body):
+    lax.fori_loop(start, stop, lambda i, _: (body(i), 0)[1], 0)
+
+
+def rows_at(i, size):
+    return pl.ds(pl.multiple_of(i * size, size), size)
+
+
+def normalise(values):
+    centre = values - jnp.mean(values, -1, keepdims=True)
+    scale = lax.rsqrt(jnp.mean(centre * centre, -1, keepdims=True) + NORM_EPS)
+    return centre * scale, scale
+
+
+def normalise_back(unit, scale, grad):
+    return scale * (grad - jnp.mean(grad, -1, keepdims=True) - unit * jnp.mean(grad * unit, -1, keepdims=True))
+
+
+def att_head(q, k, v, hot, mask):
+    n = k.shape[1]
+    k32 = k.astype(F32) * C2
+    high = k32.astype(BF)
+    low = (k32 - high.astype(F32)).astype(BF)
+    keys = jnp.concatenate([high, low, hot], 0).T
+    values = jnp.concatenate([v, jnp.ones((16, n), BF)], 0)
+    scores = mm(keys, jnp.concatenate([q, q, mask], 0))
+    e = jnp.exp2(scores - jnp.max(scores, 0, keepdims=True)).astype(BF)
+    o = mm(values, e)
+    inv = 1.0 / o[48:49]
+    return o[:48] * inv, e, inv
+
+
+def att_back_head(q, k, v, o, do, e_ref, inv):
+    n = k.shape[1]
+    values = jnp.concatenate([v, v, jnp.ones((32, n), BF)], 0).T
+    do = do.astype(F32)
+    minus = -jnp.sum(do * o, 0, keepdims=True) * inv
+    do = do * inv
+    high = do.astype(BF)
+    low = (do - high.astype(F32)).astype(BF)
+    minus_high = minus.astype(BF).astype(F32)
+    row = lax.broadcasted_iota(jnp.int32, (32, n), 0)
+    extra = jnp.where(row == 0, minus_high, jnp.where(row == 1, minus - minus_high, 0.0)).astype(BF)
+    grads = jnp.concatenate([high, low, extra], 0)
+    dq = []
+    half = n // 2
+    for t in range(2):
+        at = slice(t * half, (t + 1) * half)
+        e = e_ref[:, at]
+        ds = (e.astype(F32) * mm(values, grads[:, at])).astype(BF)
+        a = mm_nt(q[:, at], ds)
+        b = mm_nt(high[:, at], e)
+        dk, dv = (a, b) if t == 0 else (dk + a, dv + b)
+        dq.append(mm(k, ds))
+    return (jnp.concatenate(dq, 1) * SCALE).astype(BF), (dk * SCALE).astype(BF), dv.astype(BF)
+
+
+def step_kernel(*refs):
+    it = iter(refs)
+    (x, cot, pflat, seg) = (next(it) for _ in range(4))
+    (out_hbm, gin_hbm, flat, norm, e1_hbm, e2_hbm) = (next(it) for _ in range(6))
+    (net, r1, s2, r2, vec, vflat, vg, vr1, vr2, nb, nb2) = (next(it) for _ in range(11))
+    (wqkv, wself, wquery, wkv, wcross, wup, wdown) = (next(it) for _ in range(7))
+    (at, qkv, o1, h, n2t, n3t, cq, kv, far, o2) = (next(it) for _ in range(10))
+    (n4t, zt, du, dffn, dh, dcr, dot, dkv, dkv_far) = (next(it) for _ in range(9))
+    (ring, inv1, inv2, hot1, hot2, mask, stage16, stage32) = (next(it) for _ in range(8))
+    (as1, ar1, as2, ar2, bs1, br1, bs2, br2, ks, kr, vs, vr, ns, nr, es, os, gs) = (next(it) for _ in range(17))
+    j = lax.axis_index("frames")
+    b = lax.axis_index("branch")
+    z, p = j // 4, j % 4
+
+    def zp(k):
+        return (z + k) % 4 * 4 + p
+
+    def pp(k):
+        return z * 4 + (p + k) % 4
+
+    bar = pltpu.get_barrier_semaphore()
+    for k in (1, 2, 3):
+        pl.semaphore_signal(bar, inc=1, device_id={"frames": zp(k)}, device_id_type=MESH)
+        pl.semaphore_signal(bar, inc=1, device_id={"frames": pp(k)}, device_id_type=MESH)
+    for k in range(4):
+        pl.semaphore_signal(bar, inc=1, device_id={"branch": 1 - b, "frames": pp(k)}, device_id_type=MESH)
+
+    net[z, p, pl.ds(0, 16), :] = jnp.concatenate([pflat[pl.ds(1152, 8), :], jnp.zeros((8, 128), F32)], 0).astype(BF)
+    for m in range(18):
+        pair = [pflat[pl.ds(mat[0] + c, 24, stride=mat[1]), :] for mat, c in OUT_ORDER[2 * m : 2 * m + 2]]
+        net[z, p, pl.ds(LEAD + 48 * m, 48), :] = jnp.concatenate(pair, 0).astype(BF)
+    for c in range(3):
+        net[z, p, pl.ds(DOWN + 96 * c, 96), :] = pflat[pl.ds(864 + c, 96, stride=3), :].astype(BF)
+    pl.semaphore_wait(bar, 10)
+
+    a1, a2, b1, b2 = {}, {}, {}, {}
+
+    def out_first(i):
+        part = net.at[z, p, pl.ds(*OUT_PIECES[i])]
+        for k in (1, 2, 3):
+            a1[i, k] = remote(part, part, as1.at[i, k - 1], ar1.at[i, k - 1], frames=zp(k))
+            a1[i, k].start()
+
+    def out_second(i):
+        for k in (1, 2, 3):
+            a1[i, k].wait_recv()
+        part = net.at[:, p, pl.ds(*OUT_PIECES[i])]
+        for k in (1, 2, 3):
+            a2[i, k] = remote(part, part, as2.at[i, k - 1], ar2.at[i, k - 1], frames=pp(k))
+            a2[i, k].start()
+
+    def out_ready(i):
+        for k in (1, 2, 3):
+            a2[i, k].wait_recv()
+
+    def back_first(i):
+        rows = pl.ds(*BACK_PIECES[i])
+        for k in (1, 2, 3):
+            b1[i, k] = remote(
+                net.at[:, (p + k) % 4, rows], r1.at[k - 1, :, rows], bs1.at[i, k - 1], br1.at[i, k - 1], frames=pp(k)
+            )
+            b1[i, k].start()
+
+    def back_second(i):
+        rows = pl.ds(*BACK_PIECES[i])
+        for k in (1, 2, 3):
+            b1[i, k].wait_recv()
+        for k in (1, 2, 3, 0):
+            to = (z + k) % 4
+            total = net[to, p, rows, :].astype(F32)
+            for q in range(3):
+                total = total + r1[q, to, rows, :].astype(F32)
+            if k:
+                s2[k - 1, rows, :] = total.astype(BF)
+                b2[i, k] = remote(
+                    s2.at[k - 1, rows], r2.at[k - 1, rows], bs2.at[i, k - 1], br2.at[i, k - 1], frames=zp(k)
+                )
+                b2[i, k].start()
+            else:
+                b2[i, 0] = total
+
+    def back_ready(i):
+        first, count = BACK_PIECES[i]
+        for k in (1, 2, 3):
+            b2[i, k].wait_recv()
+        total = b2[i, 0]
+        for k in range(3):
+            total = total + r2[k, pl.ds(first, count), :].astype(F32)
+        if first == DOWN:
+            for c in range(3):
+                flat[pl.ds(864 + c, 96, stride=3), :] = total[96 * c : 96 * c + 96]
+        else:
+            for c in range(count // 24):
+                mat, col = BACK_ORDER[(first - LEAD) // 24 + c]
+                flat[pl.ds(mat[0] + col, 24, stride=mat[1]), :] = total[24 * c : 24 * c + 24]
+        return jnp.sum((total * total).reshape(count // 8, 8, 128), 0)
+
+    def block_pair(m):
+        got = net[:, :, pl.ds(LEAD + 48 * m, 48), :].astype(F32).reshape(16, 48, 128)
+        return got[:, :24].reshape(384, 128).astype(BF), got[:, 24:].reshape(384, 128).astype(BF)
+
+    weights = {QKV: wqkv, SELF: wself, QUERY: wquery, KEYVAL: wkv, CROSS: wcross, UP: wup}
+
+    def unpack_pairs(start, stop):
+        for m in range(start, stop):
+            for (mat, c), block in zip(OUT_ORDER[2 * m : 2 * m + 2], block_pair(m)):
+                if mat in (QKV, QUERY, KEYVAL):
+                    weights[mat][pl.ds(128 * c, 128), :] = block.T
+                else:
+                    weights[mat][:, pl.ds(128 * c, 128)] = block
+
+    def put_pair(first_row, left, right):
+        both = jnp.concatenate([left.reshape(16, 24, 128), right.reshape(16, 24, 128)], 1)
+        net[:, :, pl.ds(first_row, 48), :] = both.astype(BF).reshape(4, 4, 48, 128)
+
+    for i in range(3):
+        out_first(i)
+    own = seg[pl.ds(b, 1), :]
+    other = seg[pl.ds(1 - b, 1), :]
+    number = lax.broadcasted_iota(jnp.int32, (32, N), 0)
+    same = number + 4 * j == own
+    hot1[...] = jnp.where(same, 1.0, 0.0).astype(BF)
+    hot2[...] = jnp.where(number + 4 * j == other, 1.0, 0.0).astype(BF)
+    mask[...] = jnp.where(same | (number >= 4), 0.0, MASKED).astype(BF)
+    vg[...] = jnp.zeros((16, D), F32)
+    for i in range(3):
+        out_second(i)
+    out_first(3)
+    for i in range(3):
+        out_ready(i)
+
+    vflat[...] = jnp.zeros((48, 128), F32)
+    lane = lax.broadcasted_iota(jnp.int32, (8, 128), 1)
+    sub = lax.broadcasted_iota(jnp.int32, (8, 128), 0)
+    for i in range(16):
+        got = net[i // 4, i % 4, pl.ds(0, 16), :].astype(F32)[:8]
+        got = jnp.where(sub * 128 + lane < 264, got, 0.0)
+        if i:
+            got = pltpu.roll(got, 8 * i, 1)
+            got = jnp.where(lane < 8 * i, pltpu.roll(got, 1, 0), got)
+        vflat[pl.ds(2 * i, 8), :] += got
+    for c in range(3):
+        vec[:, pl.ds(128 * c, 128)] = vflat[pl.ds(c, 16, stride=3), :]
+    unpack_pairs(0, 5)
+    wself[:, pl.ds(0, 128)] = block_pair(4)[1]
+
+    def vector(i):
+        return vec[pl.ds(i, 1), :]
+
+    def add_vector(i, grad):
+        vg[pl.ds(i, 1), :] += jnp.sum(grad, 0, keepdims=True)
+
+    def first_norm(t):
+        rows = rows_at(t, TILE)
+        unit, _ = normalise(x[rows, :].astype(F32))
+        at[:, rows] = (unit * vector(0) + vector(1)).astype(BF).T
+
+    loop(0, 4, first_norm)
+
+    def project(w, n_ref, to):
+        def part(i):
+            rows = rows_at(i, D)
+            to[rows, :] = mm(w[rows, :], n_ref[...]).astype(BF)
+
+        loop(0, to.shape[0] // D, part)
+
+    project(wqkv, at, qkv)
+    out_second(3)
+    out_first(4)
+
+    def head(ref, first, i):
+        return ref[pl.ds(pl.multiple_of(first + i * 48, 16), 48), :]
+
+    def set_head(ref, first, i, value):
+        ref[pl.ds(pl.multiple_of(first + i * 48, 16), 48), :] = value
+
+    def e_out(e_hbm, i):
+        return pltpu.make_async_copy(ring.at[i % 3], e_hbm.at[i], es.at[i % 3])
+
+    def e_in(e_hbm, i):
+        return pltpu.make_async_copy(e_hbm.at[i], ring.at[i % 3], es.at[i % 3])
+
+    def attend_heads(start, stop, q, kvs, kfirst, hot, o_ref, inv_ref, e_hbm):
+        def one(i):
+            @pl.when(i >= 3)
+            def _():
+                e_out(e_hbm, i - 3).wait()
+
+            o, e, inv = att_head(
+                head(q, 0, i), head(kvs, kfirst, i), head(kvs, kfirst + D, i), hot[...], mask[...]
+            )
+            ring[i % 3] = e
+            e_out(e_hbm, i).start()
+            set_head(o_ref, 0, i, o)
+            inv_ref[pl.ds(i, 1), :] = inv
+
+        loop(start, stop, one)
+        if stop == HEADS:
+            for i in range(5, 8):
+                e_out(e_hbm, i).wait()
+
+    def attend_back_heads(start, stop, q, kvs, kfirst, o_ref, inv_ref, e_hbm, dk_ref, dfirst):
+        if start == 0:
+            e_in(e_hbm, 0).start()
+            e_in(e_hbm, 1).start()
+
+        def one(i):
+            @pl.when(i + 2 < HEADS)
+            def _():
+                e_in(e_hbm, i + 2).start()
+
+            e_in(e_hbm, i).wait()
+            dq, dk, dv = att_back_head(
+                head(q, 0, i), head(kvs, kfirst, i), head(kvs, kfirst + D, i), head(o_ref, 0, i), head(dot, 0, i),
+                ring.at[i % 3], inv_ref[pl.ds(i, 1), :],
+            )
+            set_head(q, 0, i, dq)
+            set_head(dk_ref, dfirst, i, dk)
+            set_head(dk_ref, dfirst + D, i, dv)
+
+        loop(start, stop, one)
+
+    attend_heads(0, 4, qkv, qkv, D, hot1, o1, inv1, e1_hbm)
+    out_second(4)
+    out_first(5)
+    attend_heads(4, 8, qkv, qkv, D, hot1, o1, inv1, e1_hbm)
+    out_second(5)
+    out_ready(3)
+    unpack_pairs(5, 12)
+
+    def second_norm(t):
+        rows = rows_at(t, TILE)
+        self_out = mm(o1[:, rows].astype(BF).T, wself[...])
+        hidden = x[rows, :].astype(F32) + vector(8) * self_out
+        h[rows, :] = hidden
+        unit, _ = normalise(hidden)
+        n2t[:, rows] = (unit * vector(2) + vector(3)).astype(BF).T
+        n3t[:, rows] = (unit * vector(4) + vector(5)).astype(BF).T
+
+    loop(0, 4, second_norm)
+    project(wkv, n3t, kv)
+    send_kv = remote(kv, far, ks.at[0], kr.at[0], branch=1 - b)
+    send_kv.start()
+    project(wquery, n2t, cq)
+    send_kv.wait_recv()
+    attend_heads(0, 8, cq, far, 0, hot2, o2, inv2, e2_hbm)
+    out_ready(4)
+    unpack_pairs(12, 18)
+    out_ready(5)
+    for c in range(3):
+        wdown[:, pl.ds(128 * c, 128)] = net[:, :, pl.ds(DOWN + 96 * c, 96), :].reshape(1536, 128)
+    for c in list(a1.values()) + list(a2.values()):
+        c.wait_send()
+
+    def out_copy(t):
+        return pltpu.make_async_copy(stage16.at[t % 2], out_hbm.at[rows_at(t, TILE)], os.at[t % 2])
+
+    def feed_forward(t):
+        rows = rows_at(t, TILE)
+        cross_out = mm(o2[:, rows].astype(BF).T, wcross[...])
+        second_h = h[rows, :] + vector(9) * cross_out
+        unit, scale = normalise(second_h)
+        n4 = (unit * vector(6) + vector(7)).astype(BF)
+        n4t[:, rows] = n4.T
+        grad_out = cot[rows, :].astype(F32)
+        dffn16 = (grad_out * vector(10)).astype(BF)
+        dffn[rows, :] = dffn16
+        ffn_out = jnp.zeros((TILE, D), F32)
+        dn4 = jnp.zeros((TILE, D), F32)
+        for c in range(4):
+            part = slice(c * D, (c + 1) * D)
+            u = mm(n4, wup[:, part])
+            share = 0.5 * (1.0 + lax.erf(u * math.sqrt(0.5)))
+            slope = share + u * (jnp.exp(-0.5 * u * u) * (1.0 / math.sqrt(2.0 * math.pi)))
+            z16 = (u * share).astype(BF)
+            zt[part, rows] = z16.T
+            ffn_out = ffn_out + mm(z16, wdown[part, :])
+            du16 = (mm_nt(dffn16, wdown[part, :]) * slope).astype(BF)
+            du[rows, part] = du16
+            dn4 = dn4 + mm_nt(du16, wup[:, part])
+
+        @pl.when(t >= 2)
+        def _():
+            out_copy(t - 2).wait()
+
+        stage16[t % 2] = (second_h + vector(10) * ffn_out).astype(BF)
+        out_copy(t).start()
+        add_vector(10, grad_out * ffn_out)
+        add_vector(6, dn4 * unit)
+        add_vector(7, dn4)
+        dh2 = grad_out + normalise_back(unit, scale, dn4 * vector(6))
+        dh[rows, :] = dh2
+        add_vector(9, dh2 * cross_out)
+        dcross16 = (dh2 * vector(9)).astype(BF)
+        dcr[rows, :] = dcross16
+        dot[:, rows] = mm_nt(wcross[...], dcross16).astype(BF)
+
+    loop(0, 4, feed_forward)
+    for i in (2, 3):
+        out_copy(i).wait()
+
+    def down_grad(i):
+        grad = mm(zt[rows_at(i, D), :], dffn[...])
+        for c in range(3):
+            net[i, :, pl.ds(DOWN + 96 * c, 96), :] = grad[:, 128 * c : 128 * c + 128].astype(BF).reshape(4, 96, 128)
+
+    loop(0, 4, down_grad)
+    back_first(0)
+
+    def up_grad(i):
+        grad = mm(n4t[...], du[:, rows_at(i, 256)])
+        put_pair(pl.multiple_of(LEAD + 24 * 24 + 48 * i, 16), grad[:, :128], grad[:, 128:])
+
+    loop(0, 6, up_grad)
+    back_first(1)
+    attend_back_heads(0, 4, cq, far, 0, o2, inv2, e2_hbm, dkv, 0)
+    back_second(0)
+    attend_back_heads(4, 8, cq, far, 0, o2, inv2, e2_hbm, dkv, 0)
+    send_dkv = remote(dkv, dkv_far, ks.at[1], kr.at[1], branch=1 - b)
+    send_dkv.start()
+    back_second(1)
+    g_query = mm_nt(n2t[...], cq[...])
+    g_cross = mm(o2[...].astype(BF), dcr[...])
+    put_pair(LEAD + 24 * 12, g_query[:, :128], g_query[:, 128:256])
+    put_pair(LEAD + 24 * 22, g_cross[:, 128:256], g_cross[:, 256:])
+    send_dkv.wait_recv()
+
+    def third_back(t):
+        rows = rows_at(t, TILE)
+        dn2 = mm(cq[:, rows].T, wquery[...])
+        dn3 = mm(dkv_far[:, rows].T, wkv[...])
+        unit, scale = normalise(h[rows, :])
+        add_vector(2, dn2 * unit)
+        add_vector(3, dn2)
+        add_vector(4, dn3 * unit)
+        add_vector(5, dn3)
+        hidden_grad = dh[rows, :] + normalise_back(unit, scale, dn2 * vector(2) + dn3 * vector(4))
+        dh[rows, :] = hidden_grad
+        self_out = mm(o1[:, rows].astype(BF).T, wself[...])
+        add_vector(8, hidden_grad * self_out)
+        dself16 = (hidden_grad * vector(8)).astype(BF)
+        dcr[rows, :] = dself16
+        dot[:, rows] = mm_nt(wself[...], dself16).astype(BF)
+
+    g_kv = mm_nt(n3t[...], dkv_far[...])
+    put_pair(LEAD + 24 * 14, g_query[:, 256:], g_kv[:, :128])
+    put_pair(LEAD + 24 * 16, g_kv[:, 128:256], g_kv[:, 256:384])
+    put_pair(LEAD + 24 * 18, g_kv[:, 384:512], g_kv[:, 512:640])
+    put_pair(LEAD + 24 * 20, g_kv[:, 640:], g_cross[:, :128])
+    back_first(2)
+    loop(0, 4, third_back)
+    g_self = mm(o1[...].astype(BF), dcr[...])
+    squares = back_ready(0)
+    for s, (start, stop) in enumerate(((0, 3), (3, 6), (6, 8))):
+        attend_back_heads(start, stop, qkv, qkv, D, o1, inv1, e1_hbm, qkv, D)
+        g = [mm_nt(at[...], qkv[pl.ds(D * i + 128 * s, 128), :]) for i in range(3)]
+        put_pair(LEAD + 96 * s, g[0], g[1])
+        put_pair(LEAD + 96 * s + 48, g[2], g_self[:, 128 * s : 128 * s + 128])
+        back_first(3 + s)
+        back_second(2 + s)
+        if s == 0:
+            squares = squares + back_ready(1)
+        if s == 1:
+            squares = squares + back_ready(2)
+
+    def gin_copy(t):
+        return pltpu.make_async_copy(stage32.at[t % 2], gin_hbm.at[rows_at(t, TILE)], gs.at[t % 2])
+
+    def first_back(t):
+        rows = rows_at(t, TILE)
+        dn1 = mm(qkv[:, rows].T, wqkv[...])
+        unit, scale = normalise(x[rows, :].astype(F32))
+        add_vector(0, dn1 * unit)
+        add_vector(1, dn1)
+
+        @pl.when(t >= 2)
+        def _():
+            gin_copy(t - 2).wait()
+
+        stage32[t % 2] = dh[rows, :] + normalise_back(unit, scale, dn1 * vector(0))
+        gin_copy(t).start()
+
+    loop(0, 4, first_back)
+    v1, v2 = [], []
+    for k in (1, 2, 3):
+        v1.append(remote(vg, vr1.at[k - 1], vs.at[0, k - 1], vr.at[0, k - 1], frames=pp(k)))
+        v1[-1].start()
+    back_second(5)
+    for c in v1:
+        c.wait()
+    vg[...] = vg[...] + vr1[0] + vr1[1] + vr1[2]
+    for k in (1, 2, 3):
+        v2.append(remote(vg, vr2.at[k - 1], vs.at[1, k - 1], vr.at[1, k - 1], frames=zp(k)))
+        v2[-1].start()
+    for i in (3, 4, 5):
+        squares = squares + back_ready(i)
+    for c in v2:
+        c.wait()
+    total = vg[...] + vr2[0] + vr2[1] + vr2[2]
+    for c in range(3):
+        vflat[pl.ds(c, 16, stride=3), :] = total[:, 128 * c : 128 * c + 128]
+    near = vflat[pl.ds(2 * j, 8), :]
+    turn = (128 - 8 * j) % 128
+    near = pltpu.roll(near, turn, 1)
+    near = jnp.where(lane < 128 - 8 * j, near, pltpu.roll(near, 7, 0))
+    near = jnp.where(sub * 128 + lane < 264, near, 0.0)
+    flat[pl.ds(1152, 8), :] = near
+    squares = squares + near * near
+    me = 2 * p + b
+    nb[pl.ds(me, 1)] = squares[None]
+    cn, cz = [], []
+    for k in range(4):
+        for c in (0, 1):
+            if k or c:
+                i = len(cn)
+                cn.append(
+                    remote(nb.at[me], nb.at[me], ns.at[i], nr.at[i], frames=pp(k), branch=(b + c) % 2)
+                )
+                cn[-1].start()
+    for c in cn:
+        c.wait_recv()
+    nb2[pl.ds(z, 1)] = jnp.sum(nb[...], 0)[None]
+    for k in (1, 2, 3):
+        cz.append(remote(nb2.at[z], nb2.at[z], ns.at[6 + k], nr.at[6 + k], frames=zp(k)))
+        cz[-1].start()
+    for c in cz:
+        c.wait_recv()
+    norm[...] = jnp.sum(nb2[...], 0)
+    for c in [v for key, v in list(b1.items()) + list(b2.items()) if key[1]] + cn + cz + [send_kv, send_dkv]:
+        c.wait_send()
+    for i in (2, 3):
+        gin_copy(i).wait()
+
+
+def step(x, cot, pflat, seg):
+    dma = pltpu.SemaphoreType.DMA
+    v = pltpu.VMEM
+    whole = pl.BlockSpec(memory_space=v)
+    hbm = pl.BlockSpec(memory_space=pl.ANY)
+    shape = jax.ShapeDtypeStruct
+    n_out, n_back = len(OUT_PIECES), len(BACK_PIECES)
+    return pl.pallas_call(
+        step_kernel,
+        out_shape=(
+            shape((N, D), BF), shape((N, D), F32), shape((FLAT, 128), F32), shape((8, 128), F32),
+            shape((HEADS, N, N), BF), shape((HEADS, N, N), BF),
+        ),
+        in_specs=[whole] * 4,
+        out_specs=(hbm, hbm, whole, whole, hbm, hbm),
+        scratch_shapes=[
+            v((4, 4, ROWS, 128), BF), v((3, 4, ROWS, 128), BF), v((3, ROWS, 128), BF), v((3, ROWS, 128), BF),
+            v((16, D), F32), v((48, 128), F32), v((16, D), F32), v((3, 16, D), F32), v((3, 16, D), F32),
+            v((8, 8, 128), F32), v((4, 8, 128), F32),
+            v((3 * D, D), BF), v((D, D), BF), v((D, D), BF), v((2 * D, D), BF), v((D, D), BF), v((D, FF), BF),
+            v((FF, D), BF),
+            v((D, N), BF), v((3 * D, N), BF), v((D, N), F32), v((N, D), F32), v((D, N), BF), v((D, N), BF),
+            v((D, N), BF), v((2 * D, N), BF), v((2 * D, N), BF), v((D, N), F32),
+            v((D, N), BF), v((FF, N), BF), v((N, FF), BF), v((N, D), BF), v((N, D), F32), v((N, D), BF),
+            v((D, N), BF), v((2 * D, N), BF), v((2 * D, N), BF),
+            v((3, N, N), BF), v((HEADS, N), F32), v((HEADS, N), F32), v((32, N), BF), v((32, N), BF), v((32, N), BF),
+            v((2, TILE, D), BF), v((2, TILE, D), F32),
+            dma((n_out, 3)), dma((n_out, 3)), dma((n_out, 3)), dma((n_out, 3)),
+            dma((n_back, 3)), dma((n_back, 3)), dma((n_back, 3)), dma((n_back, 3)),
+            dma((2,)), dma((2,)), dma((2, 3)), dma((2, 3)), dma((10,)), dma((10,)), dma((3,)), dma((2,)), dma((2,)),
+        ],
+        compiler_params=pltpu.CompilerParams(
+            collective_id=0, has_side_effects=True, vmem_limit_bytes=63 * 1024 * 1024
+        ),
+        name="step",
+    )(x, cot, pflat, seg)
+
+
+def fast_device(frames_in, seg_ids, cotangent, params, first_moment, second_moment):
+    count = lax.axis_size("frames")
+    size = params.shape[1]
+    pflat = jnp.pad(params[0], (0, FLAT * 128 - size)).reshape(FLAT, 128)
+    result, input_grad, flat, square, _, _ = step(frames_in[0], cotangent[0], pflat, seg_ids)
+    grad_norm = jnp.sqrt(jnp.sum(square))
+    reduced = flat.reshape(1, -1)[:, :size]
+    total_params = size * count
+    total_rows = frames_in.shape[1] * count
+    threshold = 0.01 * math.sqrt(2.0 * total_params * total_rows)
+    clipped = reduced * jnp.minimum(1.0, threshold / grad_norm)
+    vector_grad = clipped[:, size - NV * D // count :]
+    first_new = BETA_ONE * first_moment + (1.0 - BETA_ONE) * clipped
+    second_new = BETA_TWO * second_moment + (1.0 - BETA_TWO) * clipped * clipped
+    mean_hat = first_new / (1.0 - BETA_ONE**STEP)
+    square_hat = second_new / (1.0 - BETA_TWO**STEP)
+    new_params = params - LEARN_RATE * (
+        mean_hat / (jnp.sqrt(square_hat) + ADAM_EPS) + DECAY_RATE * params
+    )
+    return (result[None], input_grad[None], clipped, vector_grad, grad_norm, first_new, second_new, new_params)
+
+
 def solution(mesh):
     placed = (
         P("branch", "frames", None),
@@ -248,7 +833,7 @@
         P("branch", "frames"),
     )
     return jax.shard_map(
-        on_device,
+        fast_device if mesh.shape["frames"] == 16 else on_device,
         mesh=mesh,
         in_specs=placed,
         out_specs=(

time: 1040 us -> 190 us (0.18)
  waiting for transfers between devices: 454 us -> 0 us
  matrix products: 257 us -> 0 us
  Pallas kernels: 0 us -> 167 us
  local copies, waits for them, and re-layouts: 146 us -> 6.19 us
  other arithmetic: 118 us -> 14.4 us
  blocking collectives: 39.8 us -> 0 us
  between operations: 18.8 us -> 2.51 us
    unnamed x4 -> x0, waiting for transfers between devices: 454 us -> none
    dot_general x33 -> x0, matrix products: 257 us -> none  [the longest x2 44.7 us: attend_back(): jnp.einsum('qhe,khe->hqk', grad_out, values_in, preferred_element_type=jn...]
    pallas_call x0 -> x1, Pallas kernels: none -> 167 us  [step(): pl.pallas_call(step_kernel, out_shape=(shape((N, D), BF), shape((N, D), F...]
    convert_element_type x6 -> x0, other arithmetic: 64.6 us -> none  [the longest x2 56.7 us: attend_back(): grad_scores = (probs * centred).astype(jnp.bfloat16)]
    reshape x24 -> x1, local copies, waits for them, and re-layouts: 60.9 us -> 0.86 us  [fast_device(): pflat = jnp.pad(params[0], (0, FLAT * 128 - size)).reshape(FLAT, 128)]
    unnamed x225 -> x4, local copies, waits for them, and re-layouts: 47.2 us -> 4.74 us
    psum x1 -> x0, blocking collectives: 39.8 us -> none  [on_device(): square_sum = lax.psum(local_square, ('branch', 'frames'))]
    reduce_sum x13 -> x1, other arithmetic: 40.4 us -> 1.29 us  [fast_device(): grad_norm = jnp.sqrt(jnp.sum(square))]
  transfers between devices with their start and end apart: 4 -> 0, of which waited for: 2 -> 0; matrix products, arithmetic and copies ran while one was open for 5% -> 0% of each run, Pallas kernels for 0% -> 0%
where the time goes in v1:
time: 190 us
  Pallas kernels  167 us (88%)
  other arithmetic  14.4 us (8%)
  local copies, waits for them, and re-layouts  6.19 us (3%)
  between operations  2.51 us (1%)
    pallas_call x1, Pallas kernels, step(): pl.pallas_call(step_kernel, out_shape=(shape((N, D), BF), shape((N, D), F...  167 us
    unnamed x1, other arithmetic  7.06 us
    sub x1, other arithmetic, fast_device(): params - LEARN_RATE * (mean_hat / (jnp.sqrt(square_hat) + ADAM_EPS) + DEC...  6.09 us
    unnamed x4, local copies, waits for them, and re-layouts  4.74 us

profile of v1, /device:TPU:0, one launch (start us, length us, event | category | flops | bytes accessed | tf_op | source)
XLA Modules:
  0.0 190.0 jit_solution(6933841499862379547)
XLA Ops:
  0.6 7.1 %reduce = f32[147720]{0:T(1024)S(1)} reduce(f32[1,147720]{1,0:T(1,128)} %param.9, f32[]{:T(128)} %constant.35), dimensions={0}, to_apply=%param.9.reduce_sub_computation | reduce | bytes 1181764 | tf_op args[3]
  7.7 0.9 pad_bitcast_fusion.refs_2_
  8.6 166.9 %step.1 = (bf16[1024,384]{1,0:T(8,128)(2,1)}, f32[1024,384]{1,0:T(8,128)}, f32[1160,128]{1,0:T(8,128)}, f32[8,128]{1,0:T(8,128)}, bf16[8,1024,1024]{2,1,0:T(8,128)(2,1)}, /*index=5*/bf16[8,1024,1024]{2,1,0:T(8,128)(2,1)}) custom-call(bf16[1024,384]{1,0:T(8,128)(2,1)} %bitcast.8, bf16[1024,384]{1,0:T(8,128)(2,1)} %bitcast.9, ...), custom_call_target="tpu_custom_call" | custom-call | tf_op jit(solution)/shard_map/step/pallas_call | solution.py:773
  175.5 1.3 reduce_sum.9
  177.5 6.1 %multiply_subtract_fusion = (f32[1,147720]{1,0:T(1,128)}, f32[1,147720]{1,0:T(1,128)}, f32[1,147720]{1,0:T(1,128)}, f32[1,147720]{1,0:T(1,128)S(1)}) fusion(f32[1,147720]{1,0:T(1,128)} %param.9, f32[1,147720]{1,0:T(1,128)} %param.11, f32[1,147720]{1,0:T(1,128)} %param.10, f32[]{:T(128)S(6)} %min_shard_map.3, f32[1,148480]{1,0:T(1,128)} %bitcast.11), kind=kLoop, calls=%fused_computation.4 | loop fusion | flops 2363520 | bytes 4727044 | tf_op jit(solution)/shard_map/sub | solution.py:820
  183.6 0.0 copy-start
  183.6 0.6 slice.9
  184.2 2.1 %copy.16 = bf16[1,1024,384]{2,1,0:T(8,128)(2,1)} copy(bf16[1,1024,384]{2,1,0:T(8,128)(2,1)} %bitcast.10) | data formatting | bytes 1572864
  186.3 2.7 %copy.17 = f32[1,1024,384]{2,1,0:T(8,128)} copy(f32[1,1024,384]{2,1,0:T(8,128)} %bitcast.7) | data formatting | bytes 3145728
  188.9 0.0 copy-done
Async XLA Ops:
  183.6 5.3 %copy-start = (f32[1,147720]{1,0:T(1,128)}, f32[1,147720]{1,0:T(1,128)S(1)}, u32[]{:S(2)}) copy-start(f32[1,147720]{1,0:T(1,128)S(1)} %get-tuple-element.30) | copy-start | bytes 1772644

commit v2 on v1

--- a/solution.py
+++ b/solution.py
@@ -252,9 +252,9 @@
 ROWS = DOWN + 288
 FLAT = 1160
 QKV, SELF, QUERY, KEYVAL, CROSS, UP = (0, 9), (216, 3), (288, 3), (360, 6), (504, 3), (576, 12)
-OUT_ORDER = [(m, c) for m in (QKV, SELF, QUERY, KEYVAL, CROSS, UP) for c in range(m[1])]
-BACK_ORDER = [e for s in range(3) for e in ((QKV, s), (QKV, 3 + s), (QKV, 6 + s), (SELF, s))] + OUT_ORDER[12:]
-OUT_PIECES = ((0, 112), (112, 96), (208, 48), (256, 336), (592, 288), (880, 288))
+ORDER = [e for s in range(3) for e in ((QKV, s), (QKV, 3 + s), (QKV, 6 + s), (SELF, s))]
+ORDER += [(m, c) for m in (QUERY, KEYVAL, CROSS, UP) for c in range(m[1])]
+OUT_PIECES = ((0, 112), (112, 96), (208, 96), (304, 288), (592, 288), (880, 288))
 BACK_PIECES = ((880, 288), (592, 288), (304, 288), (16, 96), (112, 96), (208, 96))
 
 
@@ -290,21 +290,7 @@
     return scale * (grad - jnp.mean(grad, -1, keepdims=True) - unit * jnp.mean(grad * unit, -1, keepdims=True))
 
 
-def att_head(q, k, v, hot, mask):
-    n = k.shape[1]
-    k32 = k.astype(F32) * C2
-    high = k32.astype(BF)
-    low = (k32 - high.astype(F32)).astype(BF)
-    keys = jnp.concatenate([high, low, hot], 0).T
-    values = jnp.concatenate([v, jnp.ones((16, n), BF)], 0)
-    scores = mm(keys, jnp.concatenate([q, q, mask], 0))
-    e = jnp.exp2(scores - jnp.max(scores, 0, keepdims=True)).astype(BF)
-    o = mm(values, e)
-    inv = 1.0 / o[48:49]
-    return o[:48] * inv, e, inv
-
-
-def att_back_head(q, k, v, o, do, e_ref, inv):
+def att_back_head(q, k, v, o, do, e, inv, e_turned, ds_turned):
     n = k.shape[1]
     values = jnp.concatenate([v, v, jnp.ones((32, n), BF)], 0).T
     do = do.astype(F32)
@@ -316,17 +302,13 @@
     row = lax.broadcasted_iota(jnp.int32, (32, n), 0)
     extra = jnp.where(row == 0, minus_high, jnp.where(row == 1, minus - minus_high, 0.0)).astype(BF)
     grads = jnp.concatenate([high, low, extra], 0)
-    dq = []
-    half = n // 2
-    for t in range(2):
-        at = slice(t * half, (t + 1) * half)
-        e = e_ref[:, at]
-        ds = (e.astype(F32) * mm(values, grads[:, at])).astype(BF)
-        a = mm_nt(q[:, at], ds)
-        b = mm_nt(high[:, at], e)
-        dk, dv = (a, b) if t == 0 else (dk + a, dv + b)
-        dq.append(mm(k, ds))
-    return (jnp.concatenate(dq, 1) * SCALE).astype(BF), (dk * SCALE).astype(BF), dv.astype(BF)
+    e_turned[...] = e.T
+    ds = (e.astype(F32) * mm(values, grads)).astype(BF)
+    ds_turned[...] = ds.T
+    dq = mm(k, ds)
+    dk = mm(q, ds_turned[...])
+    dv = mm(high, e_turned[...])
+    return (dq * SCALE).astype(BF), (dk * SCALE).astype(BF), dv.astype(BF)
 
 
 def step_kernel(*refs):
@@ -337,7 +319,7 @@
     (wqkv, wself, wquery, wkv, wcross, wup, wdown) = (next(it) for _ in range(7))
     (at, qkv, o1, h, n2t, n3t, cq, kv, far, o2) = (next(it) for _ in range(10))
     (n4t, zt, du, dffn, dh, dcr, dot, dkv, dkv_far) = (next(it) for _ in range(9))
-    (ring, inv1, inv2, hot1, hot2, mask, stage16, stage32) = (next(it) for _ in range(8))
+    (ring, keys, scores, inv1, inv2, hot1, hot2, mask, stage16, stage32) = (next(it) for _ in range(10))
     (as1, ar1, as2, ar2, bs1, br1, bs2, br2, ks, kr, vs, vr, ns, nr, es, os, gs) = (next(it) for _ in range(17))
     j = lax.axis_index("frames")
     b = lax.axis_index("branch")
@@ -358,44 +340,56 @@
 
     net[z, p, pl.ds(0, 16), :] = jnp.concatenate([pflat[pl.ds(1152, 8), :], jnp.zeros((8, 128), F32)], 0).astype(BF)
     for m in range(18):
-        pair = [pflat[pl.ds(mat[0] + c, 24, stride=mat[1]), :] for mat, c in OUT_ORDER[2 * m : 2 * m + 2]]
+        pair = [pflat[pl.ds(mat[0] + c, 24, stride=mat[1]), :] for mat, c in ORDER[2 * m : 2 * m + 2]]
         net[z, p, pl.ds(LEAD + 48 * m, 48), :] = jnp.concatenate(pair, 0).astype(BF)
     for c in range(3):
         net[z, p, pl.ds(DOWN + 96 * c, 96), :] = pflat[pl.ds(864 + c, 96, stride=3), :].astype(BF)
     pl.semaphore_wait(bar, 10)
 
-    a1, a2, b1, b2 = {}, {}, {}, {}
+    others = (1, 2, 3)
+
+    def a1(i, k):
+        part = net.at[z, p, pl.ds(*OUT_PIECES[i])]
+        return remote(part, part, as1.at[i, k - 1], ar1.at[i, k - 1], frames=zp(k))
+
+    def a2(i, k):
+        part = net.at[:, p, pl.ds(*OUT_PIECES[i])]
+        return remote(part, part, as2.at[i, k - 1], ar2.at[i, k - 1], frames=pp(k))
+
+    def b1(i, k):
+        rows = pl.ds(*BACK_PIECES[i])
+        return remote(
+            net.at[:, (p + k) % 4, rows], r1.at[k - 1, :, rows], bs1.at[i, k - 1], br1.at[i, k - 1], frames=pp(k)
+        )
+
+    def b2(i, k):
+        rows = pl.ds(*BACK_PIECES[i])
+        return remote(s2.at[k - 1, rows], r2.at[k - 1, rows], bs2.at[i, k - 1], br2.at[i, k - 1], frames=zp(k))
 
     def out_first(i):
-        part = net.at[z, p, pl.ds(*OUT_PIECES[i])]
-        for k in (1, 2, 3):
-            a1[i, k] = remote(part, part, as1.at[i, k - 1], ar1.at[i, k - 1], frames=zp(k))
-            a1[i, k].start()
+        for k in others:
+            a1(i, k).start()
 
     def out_second(i):
-        for k in (1, 2, 3):
-            a1[i, k].wait_recv()
-        part = net.at[:, p, pl.ds(*OUT_PIECES[i])]
-        for k in (1, 2, 3):
-            a2[i, k] = remote(part, part, as2.at[i, k - 1], ar2.at[i, k - 1], frames=pp(k))
-            a2[i, k].start()
+        for k in others:
+            a1(i, k).wait_recv()
+        for k in others:
+            a2(i, k).start()
 
     def out_ready(i):
-        for k in (1, 2, 3):
-            a2[i, k].wait_recv()
+        for k in others:
+            a2(i, k).wait_recv()
 
     def back_first(i):
-        rows = pl.ds(*BACK_PIECES[i])
-        for k in (1, 2, 3):
-            b1[i, k] = remote(
-                net.at[:, (p + k) % 4, rows], r1.at[k - 1, :, rows], bs1.at[i, k - 1], br1.at[i, k - 1], frames=pp(k)
-            )
-            b1[i, k].start()
+        for k in others:
+            b1(i, k).start()
+
+    mine = {}
 
     def back_second(i):
         rows = pl.ds(*BACK_PIECES[i])
-        for k in (1, 2, 3):
-            b1[i, k].wait_recv()
+        for k in others:
+            b1(i, k).wait_recv()
         for k in (1, 2, 3, 0):
             to = (z + k) % 4
             total = net[to, p, rows, :].astype(F32)
@@ -403,18 +397,15 @@
                 total = total + r1[q, to, rows, :].astype(F32)
             if k:
                 s2[k - 1, rows, :] = total.astype(BF)
-                b2[i, k] = remote(
-                    s2.at[k - 1, rows], r2.at[k - 1, rows], bs2.at[i, k - 1], br2.at[i, k - 1], frames=zp(k)
-                )
-                b2[i, k].start()
+                b2(i, k).start()
             else:
-                b2[i, 0] = total
+                mine[i] = total
 
     def back_ready(i):
         first, count = BACK_PIECES[i]
-        for k in (1, 2, 3):
-            b2[i, k].wait_recv()
-        total = b2[i, 0]
+        for k in others:
+            b2(i, k).wait_recv()
+        total = mine[i]
         for k in range(3):
             total = total + r2[k, pl.ds(first, count), :].astype(F32)
         if first == DOWN:
@@ -422,7 +413,7 @@
                 flat[pl.ds(864 + c, 96, stride=3), :] = total[96 * c : 96 * c + 96]
         else:
             for c in range(count // 24):
-                mat, col = BACK_ORDER[(first - LEAD) // 24 + c]
+                mat, col = ORDER[(first - LEAD) // 24 + c]
                 flat[pl.ds(mat[0] + col, 24, stride=mat[1]), :] = total[24 * c : 24 * c + 24]
         return jnp.sum((total * total).reshape(count // 8, 8, 128), 0)
 
@@ -434,7 +425,7 @@
 
     def unpack_pairs(start, stop):
         for m in range(start, stop):
-            for (mat, c), block in zip(OUT_ORDER[2 * m : 2 * m + 2], block_pair(m)):
+            for (mat, c), block in zip(ORDER[2 * m : 2 * m + 2], block_pair(m)):
                 if mat in (QKV, QUERY, KEYVAL):
                     weights[mat][pl.ds(128 * c, 128), :] = block.T
                 else:
@@ -457,8 +448,7 @@
     for i in range(3):
         out_second(i)
     out_first(3)
-    for i in range(3):
-        out_ready(i)
+    out_ready(0)
 
     vflat[...] = jnp.zeros((48, 128), F32)
     lane = lax.broadcasted_iota(jnp.int32, (8, 128), 1)
@@ -472,8 +462,7 @@
         vflat[pl.ds(2 * i, 8), :] += got
     for c in range(3):
         vec[:, pl.ds(128 * c, 128)] = vflat[pl.ds(c, 16, stride=3), :]
-    unpack_pairs(0, 5)
-    wself[:, pl.ds(0, 128)] = block_pair(4)[1]
+    unpack_pairs(0, 2)
 
     def vector(i):
         return vec[pl.ds(i, 1), :]
@@ -495,9 +484,14 @@
 
         loop(0, to.shape[0] // D, part)
 
-    project(wqkv, at, qkv)
-    out_second(3)
-    out_first(4)
+
+    def project_round(i):
+        parts = [pl.ds(D * m + 128 * i, 128) for m in range(3)]
+        got = mm(jnp.concatenate([wqkv[part, :] for part in parts], 0), at[...]).astype(BF)
+        for m, part in enumerate(parts):
+            qkv[part, :] = got[128 * m : 128 * m + 128]
+
+    project_round(0)
 
     def head(ref, first, i):
         return ref[pl.ds(pl.multiple_of(first + i * 48, 16), 48), :]
@@ -506,44 +500,84 @@
         ref[pl.ds(pl.multiple_of(first + i * 48, 16), 48), :] = value
 
     def e_out(e_hbm, i):
-        return pltpu.make_async_copy(ring.at[i % 3], e_hbm.at[i], es.at[i % 3])
+        return pltpu.make_async_copy(ring.at[i % 2], e_hbm.at[i], es.at[i % 2])
 
     def e_in(e_hbm, i):
-        return pltpu.make_async_copy(e_hbm.at[i], ring.at[i % 3], es.at[i % 3])
-
-    def attend_heads(start, stop, q, kvs, kfirst, hot, o_ref, inv_ref, e_hbm):
-        def one(i):
-            @pl.when(i >= 3)
+        return pltpu.make_async_copy(e_hbm.at[i], ring.at[i % 2], es.at[i % 2])
+
+    half, chunk = N // 2, 256
+
+    def attend(q, kvs, kfirst, hot, o_ref, inv_ref, e_hbm, before):
+        def make_keys(i):
+            k32 = head(kvs, kfirst, i).astype(F32) * C2
+            high = k32.astype(BF)
+            low = (k32 - high.astype(F32)).astype(BF)
+            keys[i % 2] = jnp.concatenate([high, low, hot[...]], 0).T
+
+        def make_queries(i, t):
+            at_t = slice(t * half, (t + 1) * half)
+            mine = q[pl.ds(pl.multiple_of(i * 48, 16), 48), at_t]
+            return jnp.concatenate([mine, mine, mask[:, at_t]], 0)
+
+        def score(i, t, c, queries, top):
+            rows = slice(c * chunk, (c + 1) * chunk)
+            got = mm(keys[i % 2, rows, :], queries)
+            scores[t, rows, :] = got
+            got = jnp.max(got.reshape(chunk // 8, 8, half), 0)
+            return got if c == 0 else jnp.maximum(top, got)
+
+        make_keys(0)
+        top = None
+        queries = make_queries(0, 0)
+        for c in range(N // chunk):
+            top = score(0, 0, c, queries, top)
+
+        def one(i, top):
+            after = jnp.minimum(i + 1, HEADS - 1)
+            before(i)
+
+            @pl.when(i >= 2)
             def _():
-                e_out(e_hbm, i - 3).wait()
-
-            o, e, inv = att_head(
-                head(q, 0, i), head(kvs, kfirst, i), head(kvs, kfirst + D, i), hot[...], mask[...]
-            )
-            ring[i % 3] = e
+                e_out(e_hbm, i - 2).wait()
+
+            values = jnp.concatenate([head(kvs, kfirst + D, i), jnp.ones((16, N), BF)], 0)
+            for t in range(2):
+                if t:
+                    make_keys(after)
+                next_head, next_half = (after, 0) if t else (i, 1)
+                peak = jnp.max(top, 0, keepdims=True)
+                queries = make_queries(next_head, next_half)
+                at_t = slice(t * half, (t + 1) * half)
+                o = jnp.zeros((64, half), F32)
+                for c in range(N // chunk):
+                    rows = slice(c * chunk, (c + 1) * chunk)
+                    top = score(next_head, next_half, c, queries, top)
+                    e = jnp.exp2(scores[t, rows, :] - peak).astype(BF)
+                    ring[i % 2, rows, at_t] = e
+                    o = o + mm(values[:, rows], e)
+                inv = 1.0 / o[48:49]
+                o_ref[pl.ds(pl.multiple_of(i * 48, 16), 48), at_t] = o[:48] * inv
+                inv_ref[pl.ds(i, 1), at_t] = inv
             e_out(e_hbm, i).start()
-            set_head(o_ref, 0, i, o)
-            inv_ref[pl.ds(i, 1), :] = inv
-
-        loop(start, stop, one)
-        if stop == HEADS:
-            for i in range(5, 8):
-                e_out(e_hbm, i).wait()
+            return top
+
+        lax.fori_loop(0, HEADS, one, top)
+        for i in (6, 7):
+            e_out(e_hbm, i).wait()
 
     def attend_back_heads(start, stop, q, kvs, kfirst, o_ref, inv_ref, e_hbm, dk_ref, dfirst):
         if start == 0:
             e_in(e_hbm, 0).start()
-            e_in(e_hbm, 1).start()
 
         def one(i):
-            @pl.when(i + 2 < HEADS)
+            @pl.when(i + 1 < HEADS)
             def _():
-                e_in(e_hbm, i + 2).start()
+                e_in(e_hbm, i + 1).start()
 
             e_in(e_hbm, i).wait()
             dq, dk, dv = att_back_head(
                 head(q, 0, i), head(kvs, kfirst, i), head(kvs, kfirst + D, i), head(o_ref, 0, i), head(dot, 0, i),
-                ring.at[i % 3], inv_ref[pl.ds(i, 1), :],
+                ring[i % 2], inv_ref[pl.ds(i, 1), :], zt.at[pl.ds(0, N)], du.at[:, pl.ds(0, N)],
             )
             set_head(q, 0, i, dq)
             set_head(dk_ref, dfirst, i, dk)
@@ -551,13 +585,27 @@
 
         loop(start, stop, one)
 
-    attend_heads(0, 4, qkv, qkv, D, hot1, o1, inv1, e1_hbm)
-    out_second(4)
-    out_first(5)
-    attend_heads(4, 8, qkv, qkv, D, hot1, o1, inv1, e1_hbm)
+    def more_weights(i):
+        @pl.when(i == 1)
+        def _():
+            out_ready(1)
+            unpack_pairs(2, 4)
+            project_round(1)
+            out_second(3)
+            out_first(4)
+
+        @pl.when(i == 4)
+        def _():
+            out_ready(2)
+            unpack_pairs(4, 6)
+            project_round(2)
+            out_second(4)
+            out_first(5)
+
+    attend(qkv, qkv, D, hot1, o1, inv1, e1_hbm, more_weights)
     out_second(5)
     out_ready(3)
-    unpack_pairs(5, 12)
+    unpack_pairs(6, 12)
 
     def second_norm(t):
         rows = rows_at(t, TILE)
@@ -574,14 +622,16 @@
     send_kv.start()
     project(wquery, n2t, cq)
     send_kv.wait_recv()
-    attend_heads(0, 8, cq, far, 0, hot2, o2, inv2, e2_hbm)
+    attend(cq, far, 0, hot2, o2, inv2, e2_hbm, lambda i: None)
     out_ready(4)
     unpack_pairs(12, 18)
     out_ready(5)
     for c in range(3):
         wdown[:, pl.ds(128 * c, 128)] = net[:, :, pl.ds(DOWN + 96 * c, 96), :].reshape(1536, 128)
-    for c in list(a1.values()) + list(a2.values()):
-        c.wait_send()
+    for i in range(len(OUT_PIECES)):
+        for k in others:
+            a1(i, k).wait_send()
+            a2(i, k).wait_send()
 
     def out_copy(t):
         return pltpu.make_async_copy(stage16.at[t % 2], out_hbm.at[rows_at(t, TILE)], os.at[t % 2])
@@ -757,7 +807,11 @@
     for c in cz:
         c.wait_recv()
     norm[...] = jnp.sum(nb2[...], 0)
-    for c in [v for key, v in list(b1.items()) + list(b2.items()) if key[1]] + cn + cz + [send_kv, send_dkv]:
+    for i in range(len(BACK_PIECES)):
+        for k in others:
+            b1(i, k).wait_send()
+            b2(i, k).wait_send()
+    for c in cn + cz + [send_kv, send_dkv]:
         c.wait_send()
     for i in (2, 3):
         gin_copy(i).wait()
@@ -788,11 +842,11 @@
             v((D, N), BF), v((2 * D, N), BF), v((2 * D, N), BF), v((D, N), F32),
             v((D, N), BF), v((FF, N), BF), v((N, FF), BF), v((N, D), BF), v((N, D), F32), v((N, D), BF),
             v((D, N), BF), v((2 * D, N), BF), v((2 * D, N), BF),
-            v((3, N, N), BF), v((HEADS, N), F32), v((HEADS, N), F32), v((32, N), BF), v((32, N), BF), v((32, N), BF),
+            v((2, N, N), BF), v((2, N, 128), BF), v((2, N, N // 2), F32), v((HEADS, N), F32), v((HEADS, N), F32), v((32, N), BF), v((32, N), BF), v((32, N), BF),
             v((2, TILE, D), BF), v((2, TILE, D), F32),
             dma((n_out, 3)), dma((n_out, 3)), dma((n_out, 3)), dma((n_out, 3)),
             dma((n_back, 3)), dma((n_back, 3)), dma((n_back, 3)), dma((n_back, 3)),
-            dma((2,)), dma((2,)), dma((2, 3)), dma((2, 3)), dma((10,)), dma((10,)), dma((3,)), dma((2,)), dma((2,)),
+            dma((2,)), dma((2,)), dma((2, 3)), dma((2, 3)), dma((10,)), dma((10,)), dma((2,)), dma((2,)), dma((2,)),
         ],
         compiler_params=pltpu.CompilerParams(
             collective_id=0, has_side_effects=True, vmem_limit_bytes=63 * 1024 * 1024
@@ -801,26 +855,121 @@
     )(x, cot, pflat, seg)
 
 
+def finish_kernel(threshold, flat, square, params, first, second, out, grad_in, *rest):
+    (clip_o, vector_o, norm_o, first_o, second_o, params_o, out_o, grad_in_o) = rest[:8]
+    (p, m, v, c_s, tail_p, tail_m, tail_v, tail_c, o_s, g_s, big_in, big_out, tail_in, tail_out, way_in, way_out) = rest[8:]
+    size = params.shape[1]
+    main = size // 1024 * 1024
+    parts = 4
+    rows = main // 128 // parts
+    moves = []
+    for i, (src, by, dst) in enumerate(((out, o_s, out_o), (grad_in, g_s, grad_in_o))):
+        count = src.shape[0] // 2
+        for k in range(2):
+            at = pl.ds(k * count, count)
+            moves.append((
+                pltpu.make_async_copy(src.at[at], by.at[at], way_in.at[i, k]),
+                pltpu.make_async_copy(by.at[at], dst.at[at], way_out.at[i, k]),
+            ))
+    for come, _ in moves:
+        come.start()
+    reads = []
+    for i in range(parts):
+        at = pl.ds(i * rows * 128, rows * 128)
+        for k, (src, dst) in enumerate(((params, p), (first, m), (second, v))):
+            c = pltpu.make_async_copy(
+                src.at[:, at].reshape(rows, 128), dst.at[pl.ds(i * rows, rows)], big_in.at[i, k]
+            )
+            c.start()
+            reads.append(c)
+    for k, (src, dst) in enumerate(((params, tail_p), (first, tail_m), (second, tail_v))):
+        c = pltpu.make_async_copy(src.at[:, pl.ds(main, size - main)], dst, tail_in.at[k])
+        c.start()
+        reads.append(c)
+    norm = jnp.sqrt(jnp.sum(square[...], keepdims=True))
+    norm_o[...] = norm
+    share = jnp.minimum(1.0, threshold / norm)
+
+    def update(grad, p_ref, m_ref, v_ref):
+        clipped = grad * share
+        first_new = BETA_ONE * m_ref[...] + (1.0 - BETA_ONE) * clipped
+        second_new = BETA_TWO * v_ref[...] + (1.0 - BETA_TWO) * clipped * clipped
+        mean_hat = first_new / (1.0 - BETA_ONE**STEP)
+        square_hat = second_new / (1.0 - BETA_TWO**STEP)
+        old = p_ref[...]
+        p_ref[...] = old - LEARN_RATE * (mean_hat / (jnp.sqrt(square_hat) + ADAM_EPS) + DECAY_RATE * old)
+        m_ref[...] = first_new
+        v_ref[...] = second_new
+        return clipped
+
+    writes = []
+    for i in range(parts):
+        come, go = moves[i]
+        come.wait()
+        go.start()
+        writes.append(go)
+        for c in reads[3 * i : 3 * i + 3]:
+            c.wait()
+        here = pl.ds(i * rows, rows)
+        c_s[here] = update(flat[here], p.at[here], m.at[here], v.at[here])
+        at = pl.ds(i * rows * 128, rows * 128)
+        for k, (src, dst) in enumerate(((c_s, clip_o), (m, first_o), (v, second_o), (p, params_o))):
+            c = pltpu.make_async_copy(
+                src.at[here], dst.at[:, at].reshape(rows, 128), big_out.at[i, k]
+            )
+            c.start()
+            writes.append(c)
+    for c in reads[3 * parts :]:
+        c.wait()
+    wide = jnp.concatenate([flat[main // 128 + i : main // 128 + i + 1] for i in range(3)], 1)
+    tail_c[...] = update(wide[:, : size - main], tail_p, tail_m, tail_v)
+    vector_o[...] = tail_c[...]
+    for k, (src, dst) in enumerate(((tail_c, clip_o), (tail_m, first_o), (tail_v, second_o), (tail_p, params_o))):
+        c = pltpu.make_async_copy(src, dst.at[:, pl.ds(main, size - main)], tail_out.at[k])
+        c.start()
+        writes.append(c)
+    for c in writes:
+        c.wait()
+
+
+def finish(threshold, flat, square, params, first, second, out, grad_in):
+    size = params.shape[1]
+    main = size // 1024 * 1024
+    dma = pltpu.SemaphoreType.DMA
+    v = pltpu.VMEM
+    whole = pl.BlockSpec(memory_space=v)
+    hbm = pl.BlockSpec(memory_space=pl.ANY)
+    shape = jax.ShapeDtypeStruct
+    like = shape(params.shape, F32)
+    return pl.pallas_call(
+        partial(finish_kernel, threshold),
+        out_shape=(
+            like, shape((1, size - main), F32), shape((1, 1), F32), like, like, like, shape(out.shape, BF),
+            shape(grad_in.shape, F32),
+        ),
+        in_specs=[whole, whole, hbm, hbm, hbm, hbm, hbm],
+        out_specs=(hbm, whole, whole, hbm, hbm, hbm, hbm, hbm),
+        scratch_shapes=[v((main // 128, 128), F32)] * 4 + [v((1, size - main), F32)] * 4
+        + [v(out.shape, BF), v(grad_in.shape, F32)]
+        + [dma((4, 3)), dma((4, 4)), dma((3,)), dma((4,)), dma((2, 2)), dma((2, 2))],
+        name="finish",
+    )(flat, square, params, first, second, out, grad_in)
+
+
 def fast_device(frames_in, seg_ids, cotangent, params, first_moment, second_moment):
     count = lax.axis_size("frames")
     size = params.shape[1]
-    pflat = jnp.pad(params[0], (0, FLAT * 128 - size)).reshape(FLAT, 128)
+    pflat = jnp.pad(params, ((0, 0), (0, FLAT * 128 - size))).reshape(FLAT, 128)
     result, input_grad, flat, square, _, _ = step(frames_in[0], cotangent[0], pflat, seg_ids)
-    grad_norm = jnp.sqrt(jnp.sum(square))
-    reduced = flat.reshape(1, -1)[:, :size]
     total_params = size * count
     total_rows = frames_in.shape[1] * count
     threshold = 0.01 * math.sqrt(2.0 * total_params * total_rows)
-    clipped = reduced * jnp.minimum(1.0, threshold / grad_norm)
-    vector_grad = clipped[:, size - NV * D // count :]
-    first_new = BETA_ONE * first_moment + (1.0 - BETA_ONE) * clipped
-    second_new = BETA_TWO * second_moment + (1.0 - BETA_TWO) * clipped * clipped
-    mean_hat = first_new / (1.0 - BETA_ONE**STEP)
-    square_hat = second_new / (1.0 - BETA_TWO**STEP)
-    new_params = params - LEARN_RATE * (
-        mean_hat / (jnp.sqrt(square_hat) + ADAM_EPS) + DECAY_RATE * params
-    )
-    return (result[None], input_grad[None], clipped, vector_grad, grad_norm, first_new, second_new, new_params)
+    clipped, vector_grad, norm, first_new, second_new, new_params, result, input_grad = finish(
+        threshold, flat, square, params, first_moment, second_moment, result, input_grad
+    )
+    return (
+        result[None], input_grad[None], clipped, vector_grad, norm.reshape(()), first_new, second_new, new_params,
+    )
 
 
 def solution(mesh):

time: 190 us -> 168 us (0.88)
  other arithmetic: 14.4 us -> 0 us
  local copies, waits for them, and re-layouts: 6.19 us -> 2.48 us
  Pallas kernels: 167 us -> 164 us
    pallas_call x1, Pallas kernels: 167 us -> 159 us  [step(): pl.pallas_call(step_kernel, out_shape=(shape((N, D), BF), shape((N, D), F...]
    unnamed x1 -> x0, other arithmetic: 7.06 us -> none
    sub x1 -> x0, other arithmetic: 6.09 us -> none  [fast_device(): params - LEARN_RATE * (mean_hat / (jnp.sqrt(square_hat) + ADAM_EPS) + DEC...]
    pallas_call x0 -> x1, Pallas kernels: none -> 5.64 us  [finish(): pl.pallas_call(partial(finish_kernel, threshold), out_shape=(like, shape(...]
    unnamed x4 -> x0, local copies, waits for them, and re-layouts: 4.74 us -> none
    pad x0 -> x1, local copies, waits for them, and re-layouts: none -> 2.48 us  [fast_device(): pflat = jnp.pad(params, ((0, 0), (0, FLAT * 128 - size))).reshape(FLAT, 128)]
where the time goes in v2:
time: 168 us
  Pallas kernels  164 us (98%)
  local copies, waits for them, and re-layouts  2.48 us (1%)
    pallas_call x1, Pallas kernels, step(): pl.pallas_call(step_kernel, out_shape=(shape((N, D), BF), shape((N, D), F...  159 us
    pallas_call x1, Pallas kernels, finish(): pl.pallas_call(partial(finish_kernel, threshold), out_shape=(like, shape(...  5.64 us

profile of v2, /device:TPU:0, one launch (start us, length us, event | category | flops | bytes accessed | tf_op | source)
XLA Modules:
  0.0 167.8 jit_solution(3884995406788361259)
XLA Ops:
  0.6 2.5 %pad.4 = f32[1,148480]{1,0:T(1,128)} pad(f32[1,147720]{1,0:T(1,128)} %params.1, f32[]{:T(128)} %constant.2.clone.1), padding=0_0x0_760 | pad | bytes 1184804 | tf_op jit(solution)/shard_map/jit(_pad)/pad | solution.py:962
  3.1 158.8 %step.1 = (bf16[1024,384]{1,0:T(8,128)(2,1)}, f32[1024,384]{1,0:T(8,128)}, f32[1160,128]{1,0:T(8,128)}, f32[8,128]{1,0:T(8,128)}, bf16[8,1024,1024]{2,1,0:T(8,128)(2,1)}, /*index=5*/bf16[8,1024,1024]{2,1,0:T(8,128)(2,1)}) custom-call(bf16[1024,384]{1,0:T(8,128)(2,1)} %bitcast.7, bf16[1024,384]{1,0:T(8,128)(2,1)} %bitcast.8, f32[1160,128]{1,0:T(8,128)} %bitcast.6, ...), custom_call_target="tpu_custom_call" | custom-call | tf_op jit(solution)/shard_map/step/pallas_call | solution.py:827
  162.0 5.6 %finish.1 = (f32[1,147720]{1,0:T(1,128)}, f32[1,264]{1,0:T(1,128)}, f32[1,1]{1,0:T(1,128)}, f32[1,147720]{1,0:T(1,128)}, f32[1,147720]{1,0:T(1,128)}, /*index=5*...) custom-call(f32[1160,128]{1,0:T(8,128)} %get-tuple-element.20.flat, f32[8,128]{1,0:T(8,128)} %get-tuple-element.21.square, ...), custom_call_target="tpu_custom_call" | custom-call | tf_op jit(solution)/shard_map/finish/pallas_call | solution.py:944

commit v3 on v2

--- a/solution.py
+++ b/solution.py
@@ -313,14 +313,16 @@
 
 def step_kernel(*refs):
     it = iter(refs)
-    (x, cot, pflat, seg) = (next(it) for _ in range(4))
+    (x_hbm, cot_hbm, pflat, seg) = (next(it) for _ in range(4))
     (out_hbm, gin_hbm, flat, norm, e1_hbm, e2_hbm) = (next(it) for _ in range(6))
-    (net, r1, s2, r2, vec, vflat, vg, vr1, vr2, nb, nb2) = (next(it) for _ in range(11))
+    (net, r1, s2, r2, vec, vflat, vg, vg0, vsum, vr1, vr2, late, nb) = (next(it) for _ in range(13))
     (wqkv, wself, wquery, wkv, wcross, wup, wdown) = (next(it) for _ in range(7))
     (at, qkv, o1, h, n2t, n3t, cq, kv, far, o2) = (next(it) for _ in range(10))
-    (n4t, zt, du, dffn, dh, dcr, dot, dkv, dkv_far) = (next(it) for _ in range(9))
-    (ring, keys, scores, inv1, inv2, hot1, hot2, mask, stage16, stage32) = (next(it) for _ in range(10))
-    (as1, ar1, as2, ar2, bs1, br1, bs2, br2, ks, kr, vs, vr, ns, nr, es, os, gs) = (next(it) for _ in range(17))
+    (n4t, zt, du, dffn, dh, dcr, dot, dkv, dkv_far, gself) = (next(it) for _ in range(10))
+    (ring, keys, scores, inv1, inv2, hot1, hot2, mask, stage16, stage32, x, cot, sq) = (next(it) for _ in range(13))
+    (as1, ar1, as2, ar2, as3, ar3, bs1, br1, bs2, br2, bs3, br3, ks, kr, vs, vr, ls, lr, ns, nr, es, os, gs, xs) = (
+        next(it) for _ in range(24)
+    )
     j = lax.axis_index("frames")
     b = lax.axis_index("branch")
     z, p = j // 4, j % 4
@@ -338,12 +340,17 @@
     for k in range(4):
         pl.semaphore_signal(bar, inc=1, device_id={"branch": 1 - b, "frames": pp(k)}, device_id_type=MESH)
 
+    x_copy = pltpu.make_async_copy(x_hbm, x, xs.at[0])
+    cot_copy = pltpu.make_async_copy(cot_hbm, cot, xs.at[1])
+    x_copy.start()
+
+    def pack_pairs(start, stop):
+        for m in range(start, stop):
+            pair = [pflat[pl.ds(mat[0] + c, 24, stride=mat[1]), :] for mat, c in ORDER[2 * m : 2 * m + 2]]
+            net[z, p, pl.ds(LEAD + 48 * m, 48), :] = jnp.concatenate(pair, 0).astype(BF)
+
     net[z, p, pl.ds(0, 16), :] = jnp.concatenate([pflat[pl.ds(1152, 8), :], jnp.zeros((8, 128), F32)], 0).astype(BF)
-    for m in range(18):
-        pair = [pflat[pl.ds(mat[0] + c, 24, stride=mat[1]), :] for mat, c in ORDER[2 * m : 2 * m + 2]]
-        net[z, p, pl.ds(LEAD + 48 * m, 48), :] = jnp.concatenate(pair, 0).astype(BF)
-    for c in range(3):
-        net[z, p, pl.ds(DOWN + 96 * c, 96), :] = pflat[pl.ds(864 + c, 96, stride=3), :].astype(BF)
+    pack_pairs(0, 2)
     pl.semaphore_wait(bar, 10)
 
     others = (1, 2, 3)
@@ -352,15 +359,41 @@
         part = net.at[z, p, pl.ds(*OUT_PIECES[i])]
         return remote(part, part, as1.at[i, k - 1], ar1.at[i, k - 1], frames=zp(k))
 
+    beside = (p + 1 - 2 * (p % 2), (p + 2) % 4, 3 - p)
+
     def a2(i, k):
         part = net.at[:, p, pl.ds(*OUT_PIECES[i])]
-        return remote(part, part, as2.at[i, k - 1], ar2.at[i, k - 1], frames=pp(k))
+        return remote(part, part, as2.at[i, k], ar2.at[i, k], frames=z * 4 + beside[k])
+
+    def a3(i, k):
+        first, count = OUT_PIECES[i]
+        part = net.at[:, beside[k], pl.ds(first + k * (count // 2), count // 2)]
+        return remote(part, part, as3.at[i, k], ar3.at[i, k], frames=z * 4 + beside[1 - k])
+
+    direct = len(BACK_PIECES) - 1
 
     def b1(i, k):
-        rows = pl.ds(*BACK_PIECES[i])
+        first, count = BACK_PIECES[i]
+        if i == direct:
+            rows = pl.ds(first, count)
+            return remote(
+                net.at[:, beside[k], rows], r1.at[k, :, rows], bs1.at[i, k], br1.at[i, k], frames=z * 4 + beside[k]
+            )
+        way, across = k % 2, k // 2
+        rows = pl.ds(first + way * (count // 2), count // 2)
         return remote(
-            net.at[:, (p + k) % 4, rows], r1.at[k - 1, :, rows], bs1.at[i, k - 1], br1.at[i, k - 1], frames=pp(k)
+            net.at[:, beside[2 if across else way], rows], r1.at[across, :, rows], bs1.at[i, k], br1.at[i, k],
+            frames=z * 4 + beside[way],
         )
+
+    def b3(i, k):
+        first, count = BACK_PIECES[i]
+        rows = pl.ds(first + k * (count // 2), count // 2)
+        part = net.at[:, beside[1 - k], rows]
+        return remote(part, r1.at[2, :, rows], bs3.at[i, k], br3.at[i, k], frames=z * 4 + beside[1 - k])
+
+    def back_ways(i):
+        return range(3 if i == direct else 4)
 
     def b2(i, k):
         rows = pl.ds(*BACK_PIECES[i])
@@ -373,39 +406,56 @@
     def out_second(i):
         for k in others:
             a1(i, k).wait_recv()
-        for k in others:
+        for k in range(2 if i else 3):
             a2(i, k).start()
 
+    def out_third(i):
+        for k in range(2):
+            a2(i, k).wait_recv()
+        for k in range(2):
+            a3(i, k).start()
+
     def out_ready(i):
-        for k in others:
-            a2(i, k).wait_recv()
+        for k in range(2 if i else 3):
+            (a3 if i else a2)(i, k).wait_recv()
 
     def back_first(i):
-        for k in others:
+        for k in back_ways(i):
             b1(i, k).start()
 
-    mine = {}
+    def back_middle(i):
+        first, count = BACK_PIECES[i]
+        for k in back_ways(i):
+            b1(i, k).wait_recv()
+        for k in range(2):
+            rows = pl.ds(first + k * (count // 2), count // 2)
+            to = beside[1 - k]
+            for q in range(4):
+                net[q, to, rows, :] = (net[q, to, rows, :].astype(F32) + r1[1, q, rows, :].astype(F32)).astype(BF)
+            b3(i, k).start()
+
+    def plane_sum(i, to):
+        rows = pl.ds(*BACK_PIECES[i])
+        total = net[to, p, rows, :].astype(F32) + r1[0, to, rows, :].astype(F32) + r1[2, to, rows, :].astype(F32)
+        return total + r1[1, to, rows, :].astype(F32) if i == direct else total
 
     def back_second(i):
         rows = pl.ds(*BACK_PIECES[i])
+        if i == direct:
+            for k in back_ways(i):
+                b1(i, k).wait_recv()
+        else:
+            for k in range(2):
+                b3(i, k).wait_recv()
         for k in others:
-            b1(i, k).wait_recv()
-        for k in (1, 2, 3, 0):
-            to = (z + k) % 4
-            total = net[to, p, rows, :].astype(F32)
-            for q in range(3):
-                total = total + r1[q, to, rows, :].astype(F32)
-            if k:
-                s2[k - 1, rows, :] = total.astype(BF)
-                b2(i, k).start()
-            else:
-                mine[i] = total
+            s2[k - 1, rows, :] = plane_sum(i, (z + k) % 4).astype(BF)
+            b2(i, k).start()
 
     def back_ready(i):
         first, count = BACK_PIECES[i]
         for k in others:
             b2(i, k).wait_recv()
-        total = mine[i]
+        total = plane_sum(i, z)
         for k in range(3):
             total = total + r2[k, pl.ds(first, count), :].astype(F32)
         if first == DOWN:
@@ -415,7 +465,7 @@
             for c in range(count // 24):
                 mat, col = ORDER[(first - LEAD) // 24 + c]
                 flat[pl.ds(mat[0] + col, 24, stride=mat[1]), :] = total[24 * c : 24 * c + 24]
-        return jnp.sum((total * total).reshape(count // 8, 8, 128), 0)
+        sq[...] += jnp.sum((total * total).reshape(count // 8, 8, 128), 0)
 
     def block_pair(m):
         got = net[:, :, pl.ds(LEAD + 48 * m, 48), :].astype(F32).reshape(16, 48, 128)
@@ -435,8 +485,13 @@
         both = jnp.concatenate([left.reshape(16, 24, 128), right.reshape(16, 24, 128)], 1)
         net[:, :, pl.ds(first_row, 48), :] = both.astype(BF).reshape(4, 4, 48, 128)
 
-    for i in range(3):
-        out_first(i)
+    out_first(0)
+    pack_pairs(2, 6)
+    out_first(1)
+    out_first(2)
+    pack_pairs(6, 18)
+    for c in range(3):
+        net[z, p, pl.ds(DOWN + 96 * c, 96), :] = pflat[pl.ds(864 + c, 96, stride=3), :].astype(BF)
     own = seg[pl.ds(b, 1), :]
     other = seg[pl.ds(1 - b, 1), :]
     number = lax.broadcasted_iota(jnp.int32, (32, N), 0)
@@ -445,10 +500,14 @@
     hot2[...] = jnp.where(number + 4 * j == other, 1.0, 0.0).astype(BF)
     mask[...] = jnp.where(same | (number >= 4), 0.0, MASKED).astype(BF)
     vg[...] = jnp.zeros((16, D), F32)
-    for i in range(3):
-        out_second(i)
+    vg0[...] = jnp.zeros((8, D), F32)
+    sq[...] = jnp.zeros((8, 128), F32)
+    out_second(0)
     out_first(3)
+    out_second(1)
+    out_second(2)
     out_ready(0)
+    out_third(1)
 
     vflat[...] = jnp.zeros((48, 128), F32)
     lane = lax.broadcasted_iota(jnp.int32, (8, 128), 1)
@@ -475,6 +534,8 @@
         unit, _ = normalise(x[rows, :].astype(F32))
         at[:, rows] = (unit * vector(0) + vector(1)).astype(BF).T
 
+    x_copy.wait()
+    cot_copy.start()
     loop(0, 4, first_norm)
 
     def project(w, n_ref, to):
@@ -565,15 +626,15 @@
         for i in (6, 7):
             e_out(e_hbm, i).wait()
 
-    def attend_back_heads(start, stop, q, kvs, kfirst, o_ref, inv_ref, e_hbm, dk_ref, dfirst):
-        if start == 0:
-            e_in(e_hbm, 0).start()
+    def attend_back(q, kvs, kfirst, o_ref, inv_ref, e_hbm, dk_ref, dfirst, before):
+        e_in(e_hbm, 0).start()
 
         def one(i):
             @pl.when(i + 1 < HEADS)
             def _():
                 e_in(e_hbm, i + 1).start()
 
+            before(i)
             e_in(e_hbm, i).wait()
             dq, dk, dv = att_back_head(
                 head(q, 0, i), head(kvs, kfirst, i), head(kvs, kfirst + D, i), head(o_ref, 0, i), head(dot, 0, i),
@@ -583,28 +644,38 @@
             set_head(dk_ref, dfirst, i, dk)
             set_head(dk_ref, dfirst + D, i, dv)
 
-        loop(start, stop, one)
+        loop(0, HEADS, one)
+
+    def at_head(i, **steps):
+        for name, step in steps.items():
+            pl.when(i == int(name[1:]))(step)
 
     def more_weights(i):
+        @pl.when(i == 0)
+        def _():
+            out_second(3)
+            out_first(4)
+
         @pl.when(i == 1)
         def _():
             out_ready(1)
+            out_third(2)
             unpack_pairs(2, 4)
             project_round(1)
-            out_second(3)
-            out_first(4)
 
         @pl.when(i == 4)
         def _():
             out_ready(2)
+            out_third(3)
+            out_second(4)
+            out_first(5)
             unpack_pairs(4, 6)
             project_round(2)
-            out_second(4)
-            out_first(5)
 
     attend(qkv, qkv, D, hot1, o1, inv1, e1_hbm, more_weights)
+    out_ready(3)
+    out_third(4)
     out_second(5)
-    out_ready(3)
     unpack_pairs(6, 12)
 
     def second_norm(t):
@@ -621,9 +692,15 @@
     send_kv = remote(kv, far, ks.at[0], kr.at[0], branch=1 - b)
     send_kv.start()
     project(wquery, n2t, cq)
+
+    def last_weights(i):
+        @pl.when(i == 2)
+        def _():
+            out_ready(4)
+            out_third(5)
+
     send_kv.wait_recv()
-    attend(cq, far, 0, hot2, o2, inv2, e2_hbm, lambda i: None)
-    out_ready(4)
+    attend(cq, far, 0, hot2, o2, inv2, e2_hbm, last_weights)
     unpack_pairs(12, 18)
     out_ready(5)
     for c in range(3):
@@ -631,7 +708,10 @@
     for i in range(len(OUT_PIECES)):
         for k in others:
             a1(i, k).wait_send()
+        for k in range(2 if i else 3):
             a2(i, k).wait_send()
+            if i:
+                a3(i, k).wait_send()
 
     def out_copy(t):
         return pltpu.make_async_copy(stage16.at[t % 2], out_hbm.at[rows_at(t, TILE)], os.at[t % 2])
@@ -676,6 +756,7 @@
         dcr[rows, :] = dcross16
         dot[:, rows] = mm_nt(wcross[...], dcross16).astype(BF)
 
+    cot_copy.wait()
     loop(0, 4, feed_forward)
     for i in (2, 3):
         out_copy(i).wait()
@@ -694,12 +775,12 @@
 
     loop(0, 6, up_grad)
     back_first(1)
-    attend_back_heads(0, 4, cq, far, 0, o2, inv2, e2_hbm, dkv, 0)
-    back_second(0)
-    attend_back_heads(4, 8, cq, far, 0, o2, inv2, e2_hbm, dkv, 0)
+    attend_back(
+        cq, far, 0, o2, inv2, e2_hbm, dkv, 0, lambda i: at_head(i, h4=lambda: back_middle(0), h7=lambda: back_middle(1))
+    )
     send_dkv = remote(dkv, dkv_far, ks.at[1], kr.at[1], branch=1 - b)
     send_dkv.start()
-    back_second(1)
+    back_second(0)
     g_query = mm_nt(n2t[...], cq[...])
     g_cross = mm(o2[...].astype(BF), dcr[...])
     put_pair(LEAD + 24 * 12, g_query[:, :128], g_query[:, 128:256])
@@ -729,20 +810,73 @@
     put_pair(LEAD + 24 * 18, g_kv[:, 384:512], g_kv[:, 512:640])
     put_pair(LEAD + 24 * 20, g_kv[:, 640:], g_cross[:, :128])
     back_first(2)
+    back_second(1)
     loop(0, 4, third_back)
-    g_self = mm(o1[...].astype(BF), dcr[...])
-    squares = back_ready(0)
-    for s, (start, stop) in enumerate(((0, 3), (3, 6), (6, 8))):
-        attend_back_heads(start, stop, qkv, qkv, D, o1, inv1, e1_hbm, qkv, D)
-        g = [mm_nt(at[...], qkv[pl.ds(D * i + 128 * s, 128), :]) for i in range(3)]
-        put_pair(LEAD + 96 * s, g[0], g[1])
-        put_pair(LEAD + 96 * s + 48, g[2], g_self[:, 128 * s : 128 * s + 128])
-        back_first(3 + s)
-        back_second(2 + s)
-        if s == 0:
-            squares = squares + back_ready(1)
-        if s == 1:
-            squares = squares + back_ready(2)
+    gself[...] = mm(o1[...].astype(BF), dcr[...])
+    back_ready(0)
+
+    def v1(k):
+        return remote(vg, vr1.at[k - 1], vs.at[0, k - 1], vr.at[0, k - 1], frames=pp(k))
+
+    def v2(k):
+        return remote(vsum, vr2.at[k - 1], vs.at[1, k - 1], vr.at[1, k - 1], frames=zp(k))
+
+    for k in others:
+        v1(k).start()
+
+    def round_grad(i):
+        g = [mm_nt(at[...], qkv[pl.ds(D * m + 128 * i, 128), :]) for m in range(3)]
+        put_pair(LEAD + 96 * i, g[0], g[1])
+        put_pair(LEAD + 96 * i + 48, g[2], gself[:, 128 * i : 128 * i + 128])
+        back_first(3 + i)
+
+    def vectors_on():
+        for k in others:
+            v1(k).wait_recv()
+        vsum[...] = vg[...] + vr1[0] + vr1[1] + vr1[2]
+        for k in others:
+            v2(k).start()
+
+    def vectors_there():
+        for k in others:
+            v2(k).wait_recv()
+        total = vsum[...] + vr2[0] + vr2[1] + vr2[2]
+        for c in range(3):
+            vflat[pl.ds(c, 16, stride=3), :] = total[:, 128 * c : 128 * c + 128]
+
+    def ahead(i):
+        @pl.when(i == 2)
+        def _():
+            back_middle(2)
+            back_ready(1)
+
+        @pl.when(i == 3)
+        def _():
+            round_grad(0)
+            vectors_on()
+
+        @pl.when(i == 4)
+        def _():
+            back_second(2)
+
+        @pl.when(i == 5)
+        def _():
+            back_middle(3)
+            vectors_there()
+
+        @pl.when(i == 6)
+        def _():
+            round_grad(1)
+
+        @pl.when(i == 7)
+        def _():
+            back_second(3)
+            back_middle(4)
+            back_ready(2)
+
+    attend_back(qkv, qkv, D, o1, inv1, e1_hbm, qkv, D, ahead)
+    round_grad(2)
+    back_second(4)
 
     def gin_copy(t):
         return pltpu.make_async_copy(stage32.at[t % 2], gin_hbm.at[rows_at(t, TILE)], gs.at[t % 2])
@@ -751,8 +885,8 @@
         rows = rows_at(t, TILE)
         dn1 = mm(qkv[:, rows].T, wqkv[...])
         unit, scale = normalise(x[rows, :].astype(F32))
-        add_vector(0, dn1 * unit)
-        add_vector(1, dn1)
+        vg0[0:1, :] += jnp.sum(dn1 * unit, 0, keepdims=True)
+        vg0[1:2, :] += jnp.sum(dn1, 0, keepdims=True)
 
         @pl.when(t >= 2)
         def _():
@@ -762,57 +896,58 @@
         gin_copy(t).start()
 
     loop(0, 4, first_back)
-    v1, v2 = [], []
-    for k in (1, 2, 3):
-        v1.append(remote(vg, vr1.at[k - 1], vs.at[0, k - 1], vr.at[0, k - 1], frames=pp(k)))
-        v1[-1].start()
+    blocks = [vg0[r : r + 1, 128 * c : 128 * c + 128] for r in range(2) for c in range(3)]
+    late[pl.ds(j, 1)] = jnp.concatenate(blocks + [jnp.zeros((2, 128), F32)], 0)[None]
+
+    def far_vector(k):
+        return remote(late.at[j], late.at[j], ls.at[k - 1], lr.at[k - 1], frames=(j + k) % 16)
+
+    for k in range(1, 16):
+        far_vector(k).start()
     back_second(5)
-    for c in v1:
-        c.wait()
-    vg[...] = vg[...] + vr1[0] + vr1[1] + vr1[2]
-    for k in (1, 2, 3):
-        v2.append(remote(vg, vr2.at[k - 1], vs.at[1, k - 1], vr.at[1, k - 1], frames=zp(k)))
-        v2[-1].start()
-    for i in (3, 4, 5):
-        squares = squares + back_ready(i)
-    for c in v2:
-        c.wait()
-    total = vg[...] + vr2[0] + vr2[1] + vr2[2]
-    for c in range(3):
-        vflat[pl.ds(c, 16, stride=3), :] = total[:, 128 * c : 128 * c + 128]
+    back_ready(3)
+    back_ready(4)
+    for k in range(1, 16):
+        far_vector(k).wait_recv()
+    vflat[pl.ds(0, 8), :] += jnp.sum(late[...], 0)
     near = vflat[pl.ds(2 * j, 8), :]
     turn = (128 - 8 * j) % 128
     near = pltpu.roll(near, turn, 1)
     near = jnp.where(lane < 128 - 8 * j, near, pltpu.roll(near, 7, 0))
     near = jnp.where(sub * 128 + lane < 264, near, 0.0)
     flat[pl.ds(1152, 8), :] = near
-    squares = squares + near * near
-    me = 2 * p + b
-    nb[pl.ds(me, 1)] = squares[None]
-    cn, cz = [], []
-    for k in range(4):
-        for c in (0, 1):
-            if k or c:
-                i = len(cn)
-                cn.append(
-                    remote(nb.at[me], nb.at[me], ns.at[i], nr.at[i], frames=pp(k), branch=(b + c) % 2)
-                )
-                cn[-1].start()
-    for c in cn:
-        c.wait_recv()
-    nb2[pl.ds(z, 1)] = jnp.sum(nb[...], 0)[None]
-    for k in (1, 2, 3):
-        cz.append(remote(nb2.at[z], nb2.at[z], ns.at[6 + k], nr.at[6 + k], frames=zp(k)))
-        cz[-1].start()
-    for c in cz:
-        c.wait_recv()
-    norm[...] = jnp.sum(nb2[...], 0)
+    back_ready(5)
+    squares = sq[...] + near * near
+    me = 16 * b + j
+    nb[pl.ds(me, 1), 0:1, :] = jnp.sum(squares, 0, keepdims=True)[None]
+
+    def far_square(k):
+        to = (me + k) % 32
+        part = nb.at[me, pl.ds(0, 1)]
+        return remote(part, part, ns.at[k - 1], nr.at[k - 1], branch=to // 16, frames=to % 16)
+
+    for k in range(1, 32):
+        far_square(k).start()
+    for k in range(1, 32):
+        far_square(k).wait_recv()
+    norm[...] = jnp.sum(nb[:, 0, :], 0, keepdims=True)
     for i in range(len(BACK_PIECES)):
         for k in others:
+            b2(i, k).wait_send()
+        for k in back_ways(i):
             b1(i, k).wait_send()
-            b2(i, k).wait_send()
-    for c in cn + cz + [send_kv, send_dkv]:
-        c.wait_send()
+        if i != direct:
+            for k in range(2):
+                b3(i, k).wait_send()
+    for k in others:
+        v1(k).wait_send()
+        v2(k).wait_send()
+    for k in range(1, 16):
+        far_vector(k).wait_send()
+    for k in range(1, 32):
+        far_square(k).wait_send()
+    send_kv.wait_send()
+    send_dkv.wait_send()
     for i in (2, 3):
         gin_copy(i).wait()
 
@@ -827,26 +962,27 @@
     return pl.pallas_call(
         step_kernel,
         out_shape=(
-            shape((N, D), BF), shape((N, D), F32), shape((FLAT, 128), F32), shape((8, 128), F32),
+            shape((N, D), BF), shape((N, D), F32), shape((FLAT, 128), F32), shape((1, 128), F32),
             shape((HEADS, N, N), BF), shape((HEADS, N, N), BF),
         ),
-        in_specs=[whole] * 4,
+        in_specs=[hbm, hbm, whole, whole],
         out_specs=(hbm, hbm, whole, whole, hbm, hbm),
         scratch_shapes=[
             v((4, 4, ROWS, 128), BF), v((3, 4, ROWS, 128), BF), v((3, ROWS, 128), BF), v((3, ROWS, 128), BF),
-            v((16, D), F32), v((48, 128), F32), v((16, D), F32), v((3, 16, D), F32), v((3, 16, D), F32),
-            v((8, 8, 128), F32), v((4, 8, 128), F32),
+            v((16, D), F32), v((48, 128), F32), v((16, D), F32), v((8, D), F32), v((16, D), F32), v((3, 16, D), F32),
+            v((3, 16, D), F32), v((16, 8, 128), F32), v((32, 8, 128), F32),
             v((3 * D, D), BF), v((D, D), BF), v((D, D), BF), v((2 * D, D), BF), v((D, D), BF), v((D, FF), BF),
             v((FF, D), BF),
             v((D, N), BF), v((3 * D, N), BF), v((D, N), F32), v((N, D), F32), v((D, N), BF), v((D, N), BF),
             v((D, N), BF), v((2 * D, N), BF), v((2 * D, N), BF), v((D, N), F32),
             v((D, N), BF), v((FF, N), BF), v((N, FF), BF), v((N, D), BF), v((N, D), F32), v((N, D), BF),
-            v((D, N), BF), v((2 * D, N), BF), v((2 * D, N), BF),
+            v((D, N), BF), v((2 * D, N), BF), v((2 * D, N), BF), v((D, D), F32),
             v((2, N, N), BF), v((2, N, 128), BF), v((2, N, N // 2), F32), v((HEADS, N), F32), v((HEADS, N), F32), v((32, N), BF), v((32, N), BF), v((32, N), BF),
-            v((2, TILE, D), BF), v((2, TILE, D), F32),
-            dma((n_out, 3)), dma((n_out, 3)), dma((n_out, 3)), dma((n_out, 3)),
-            dma((n_back, 3)), dma((n_back, 3)), dma((n_back, 3)), dma((n_back, 3)),
-            dma((2,)), dma((2,)), dma((2, 3)), dma((2, 3)), dma((10,)), dma((10,)), dma((2,)), dma((2,)), dma((2,)),
+            v((2, TILE, D), BF), v((2, TILE, D), F32), v((N, D), BF), v((N, D), BF), v((8, 128), F32),
+            dma((n_out, 3)), dma((n_out, 3)), dma((n_out, 3)), dma((n_out, 3)), dma((n_out, 2)), dma((n_out, 2)),
+            dma((n_back, 4)), dma((n_back, 4)), dma((n_back, 3)), dma((n_back, 3)), dma((n_back, 2)), dma((n_back, 2)),
+            dma((2,)), dma((2,)), dma((2, 3)), dma((2, 3)), dma((15,)), dma((15,)), dma((31,)), dma((31,)),
+            dma((2,)), dma((2,)), dma((2,)), dma((2,)),
         ],
         compiler_params=pltpu.CompilerParams(
             collective_id=0, has_side_effects=True, vmem_limit_bytes=63 * 1024 * 1024

time: 168 us -> 160 us (0.952)
  Pallas kernels: 164 us -> 156 us
    pallas_call x1, Pallas kernels: 159 us -> 151 us  [step(): pl.pallas_call(step_kernel, out_shape=(shape((N, D), BF), shape((N, D), F...]
where the time goes in v3:
time: 160 us
  Pallas kernels  156 us (98%)
  local copies, waits for them, and re-layouts  2.48 us (2%)
    pallas_call x1, Pallas kernels, step(): pl.pallas_call(step_kernel, out_shape=(shape((N, D), BF), shape((N, D), F...  151 us
    pallas_call x1, Pallas kernels, finish(): pl.pallas_call(partial(finish_kernel, threshold), out_shape=(like, shape(...  5.64 us

profile of v3, /device:TPU:0, one launch (start us, length us, event | category | flops | bytes accessed | tf_op | source)
XLA Modules:
  0.0 159.7 jit_solution(10424529337467048506)
XLA Ops:
  0.6 2.5 %pad.4 = f32[1,148480]{1,0:T(1,128)} pad(f32[1,147720]{1,0:T(1,128)} %params.1, f32[]{:T(128)} %constant.2.clone.1), padding=0_0x0_760 | pad | bytes 1184804 | tf_op jit(solution)/shard_map/jit(_pad)/pad | solution.py:1098
  3.1 150.8 %step.1 = (bf16[1024,384]{1,0:T(8,128)(2,1)}, f32[1024,384]{1,0:T(8,128)}, f32[1160,128]{1,0:T(8,128)}, f32[1,128]{1,0:T(1,128)}, bf16[8,1024,1024]{2,1,0:T(8,128)(2,1)}, /*index=5*/bf16[8,1024,1024]{2,1,0:T(8,128)(2,1)}) custom-call(bf16[1024,384]{1,0:T(8,128)(2,1)} %bitcast.7, bf16[1024,384]{1,0:T(8,128)(2,1)} %bitcast.8, f32[1160,128]{1,0:T(8,128)} %bitcast.6, ...), custom_call_target="tpu_custom_call" | custom-call | tf_op jit(solution)/shard_map/step/pallas_call | solution.py:962
  153.9 5.6 %finish.1 = (f32[1,147720]{1,0:T(1,128)}, f32[1,264]{1,0:T(1,128)}, f32[1,1]{1,0:T(1,128)}, f32[1,147720]{1,0:T(1,128)}, f32[1,147720]{1,0:T(1,128)}, /*index=5*...) custom-call(f32[1160,128]{1,0:T(8,128)} %get-tuple-element.20.flat, f32[1,128]{1,0:T(1,128)} %get-tuple-element.21.square, ...), custom_call_target="tpu_custom_call" | custom-call | tf_op jit(solution)/shard_map/finish/pallas_call | solution.py:1080

commit v4 on v3

--- a/solution.py
+++ b/solution.py
@@ -246,7 +246,8 @@
 C2 = math.log2(math.e) / math.sqrt(HEAD_DIM)
 SCALE = 1.0 / math.sqrt(HEAD_DIM)
 N = 1024
-TILE = 256
+TILE = 512
+TILES = N // TILE
 LEAD = 16
 DOWN = LEAD + 36 * 24
 ROWS = DOWN + 288
@@ -254,7 +255,7 @@
 QKV, SELF, QUERY, KEYVAL, CROSS, UP = (0, 9), (216, 3), (288, 3), (360, 6), (504, 3), (576, 12)
 ORDER = [e for s in range(3) for e in ((QKV, s), (QKV, 3 + s), (QKV, 6 + s), (SELF, s))]
 ORDER += [(m, c) for m in (QUERY, KEYVAL, CROSS, UP) for c in range(m[1])]
-OUT_PIECES = ((0, 112), (112, 96), (208, 96), (304, 288), (592, 288), (880, 288))
+OUT_PIECES = ((0, 112), (112, 96), (208, 96), (304, 288), (592, 288), (880, 128), (1008, 160))
 BACK_PIECES = ((880, 288), (592, 288), (304, 288), (16, 96), (112, 96), (208, 96))
 
 
@@ -313,13 +314,13 @@
 
 def step_kernel(*refs):
     it = iter(refs)
-    (x_hbm, cot_hbm, pflat, seg) = (next(it) for _ in range(4))
+    (x_hbm, cot_hbm, params, seg) = (next(it) for _ in range(4))
     (out_hbm, gin_hbm, flat, norm, e1_hbm, e2_hbm) = (next(it) for _ in range(6))
     (net, r1, s2, r2, vec, vflat, vg, vg0, vsum, vr1, vr2, late, nb) = (next(it) for _ in range(13))
     (wqkv, wself, wquery, wkv, wcross, wup, wdown) = (next(it) for _ in range(7))
     (at, qkv, o1, h, n2t, n3t, cq, kv, far, o2) = (next(it) for _ in range(10))
     (n4t, zt, du, dffn, dh, dcr, dot, dkv, dkv_far, gself) = (next(it) for _ in range(10))
-    (ring, keys, scores, inv1, inv2, hot1, hot2, mask, stage16, stage32, x, cot, sq) = (next(it) for _ in range(13))
+    (ring, keys, scores, inv1, inv2, hot1, hot2, mask, stage16, stage32, x, cot, sq, praw) = (next(it) for _ in range(14))
     (as1, ar1, as2, ar2, as3, ar3, bs1, br1, bs2, br2, bs3, br3, ks, kr, vs, vr, ls, lr, ns, nr, es, os, gs, xs) = (
         next(it) for _ in range(24)
     )
@@ -342,32 +343,52 @@
 
     x_copy = pltpu.make_async_copy(x_hbm, x, xs.at[0])
     cot_copy = pltpu.make_async_copy(cot_hbm, cot, xs.at[1])
-    x_copy.start()
+    main = params.shape[1] // 1024 * 1024
+    urgent = SELF[0] + 24 * SELF[1]
+    spans = ((0, urgent * 128), (urgent * 128, params.shape[1] - urgent * 128))
+    p_copies = [
+        pltpu.make_async_copy(params.at[:, pl.ds(*span)], praw.at[:, pl.ds(*span)], xs.at[2 + i])
+        for i, span in enumerate(spans)
+    ]
+
+    pflat = flat
+
+    def lay_out(i):
+        pflat[rows_at(i, 8), :] = praw[:, pl.ds(pl.multiple_of(i * 1024, 1024), 1024)].reshape(8, 128)
+
+    for c in (*p_copies, x_copy):
+        c.start()
 
     def pack_pairs(start, stop):
         for m in range(start, stop):
             pair = [pflat[pl.ds(mat[0] + c, 24, stride=mat[1]), :] for mat, c in ORDER[2 * m : 2 * m + 2]]
             net[z, p, pl.ds(LEAD + 48 * m, 48), :] = jnp.concatenate(pair, 0).astype(BF)
 
-    net[z, p, pl.ds(0, 16), :] = jnp.concatenate([pflat[pl.ds(1152, 8), :], jnp.zeros((8, 128), F32)], 0).astype(BF)
+    p_copies[0].wait()
+    loop(0, urgent // 8, lay_out)
+    p_copies[1].wait()
+    tail = jnp.concatenate([praw[:, main:], jnp.zeros((1, 120), F32)], 1)
+    tail = [tail[:, 128 * i : 128 * i + 128] for i in range(3)]
+    net[z, p, pl.ds(0, 16), :] = jnp.concatenate(tail + [jnp.zeros((13, 128), F32)], 0).astype(BF)
     pack_pairs(0, 2)
     pl.semaphore_wait(bar, 10)
 
     others = (1, 2, 3)
 
+    beside = (p + 1 - 2 * (p % 2), (p + 2) % 4, 3 - p)
+    turned = len(OUT_PIECES) - 1
+
     def a1(i, k):
-        part = net.at[z, p, pl.ds(*OUT_PIECES[i])]
+        part = net.at[z, slice(None) if i == turned else p, pl.ds(*OUT_PIECES[i])]
         return remote(part, part, as1.at[i, k - 1], ar1.at[i, k - 1], frames=zp(k))
 
-    beside = (p + 1 - 2 * (p % 2), (p + 2) % 4, 3 - p)
-
     def a2(i, k):
-        part = net.at[:, p, pl.ds(*OUT_PIECES[i])]
+        part = net.at[z if i == turned else slice(None), p, pl.ds(*OUT_PIECES[i])]
         return remote(part, part, as2.at[i, k], ar2.at[i, k], frames=z * 4 + beside[k])
 
     def a3(i, k):
         first, count = OUT_PIECES[i]
-        part = net.at[:, beside[k], pl.ds(first + k * (count // 2), count // 2)]
+        part = net.at[z if i == turned else slice(None), beside[k], pl.ds(first + k * (count // 2), count // 2)]
         return remote(part, part, as3.at[i, k], ar3.at[i, k], frames=z * 4 + beside[1 - k])
 
     direct = len(BACK_PIECES) - 1
@@ -400,12 +421,16 @@
         return remote(s2.at[k - 1, rows], r2.at[k - 1, rows], bs2.at[i, k - 1], br2.at[i, k - 1], frames=zp(k))
 
     def out_first(i):
+        if i == turned:
+            for k in range(2):
+                a3(i, k).wait_recv()
         for k in others:
             a1(i, k).start()
 
     def out_second(i):
-        for k in others:
-            a1(i, k).wait_recv()
+        if i != turned:
+            for k in others:
+                a1(i, k).wait_recv()
         for k in range(2 if i else 3):
             a2(i, k).start()
 
@@ -416,6 +441,10 @@
             a3(i, k).start()
 
     def out_ready(i):
+        if i == turned:
+            for k in others:
+                a1(i, k).wait_recv()
+            return
         for k in range(2 if i else 3):
             (a3 if i else a2)(i, k).wait_recv()
 
@@ -486,12 +515,14 @@
         net[:, :, pl.ds(first_row, 48), :] = both.astype(BF).reshape(4, 4, 48, 128)
 
     out_first(0)
+    loop(urgent // 8, main // 1024, lay_out)
+    for c in range(3):
+        net[z, p, pl.ds(DOWN + 96 * c, 96), :] = pflat[pl.ds(864 + c, 96, stride=3), :].astype(BF)
+    out_second(turned)
     pack_pairs(2, 6)
     out_first(1)
     out_first(2)
     pack_pairs(6, 18)
-    for c in range(3):
-        net[z, p, pl.ds(DOWN + 96 * c, 96), :] = pflat[pl.ds(864 + c, 96, stride=3), :].astype(BF)
     own = seg[pl.ds(b, 1), :]
     other = seg[pl.ds(1 - b, 1), :]
     number = lax.broadcasted_iota(jnp.int32, (32, N), 0)
@@ -502,12 +533,12 @@
     vg[...] = jnp.zeros((16, D), F32)
     vg0[...] = jnp.zeros((8, D), F32)
     sq[...] = jnp.zeros((8, 128), F32)
+    out_third(turned)
     out_second(0)
     out_first(3)
     out_second(1)
     out_second(2)
     out_ready(0)
-    out_third(1)
 
     vflat[...] = jnp.zeros((48, 128), F32)
     lane = lax.broadcasted_iota(jnp.int32, (8, 128), 1)
@@ -536,7 +567,7 @@
 
     x_copy.wait()
     cot_copy.start()
-    loop(0, 4, first_norm)
+    loop(0, TILES, first_norm)
 
     def project(w, n_ref, to):
         def part(i):
@@ -595,8 +626,6 @@
 
         def one(i, top):
             after = jnp.minimum(i + 1, HEADS - 1)
-            before(i)
-
             @pl.when(i >= 2)
             def _():
                 e_out(e_hbm, i - 2).wait()
@@ -604,6 +633,7 @@
             values = jnp.concatenate([head(kvs, kfirst + D, i), jnp.ones((16, N), BF)], 0)
             for t in range(2):
                 if t:
+                    before(i)
                     make_keys(after)
                 next_head, next_half = (after, 0) if t else (i, 1)
                 peak = jnp.max(top, 0, keepdims=True)
@@ -650,32 +680,32 @@
         for name, step in steps.items():
             pl.when(i == int(name[1:]))(step)
 
-    def more_weights(i):
-        @pl.when(i == 0)
-        def _():
-            out_second(3)
-            out_first(4)
-
-        @pl.when(i == 1)
-        def _():
-            out_ready(1)
-            out_third(2)
-            unpack_pairs(2, 4)
-            project_round(1)
-
-        @pl.when(i == 4)
-        def _():
-            out_ready(2)
-            out_third(3)
-            out_second(4)
-            out_first(5)
-            unpack_pairs(4, 6)
-            project_round(2)
-
-    attend(qkv, qkv, D, hot1, o1, inv1, e1_hbm, more_weights)
+    def second_round():
+        out_ready(1)
+        out_third(2)
+        unpack_pairs(2, 4)
+        project_round(1)
+
+    def third_round():
+        out_ready(2)
+        unpack_pairs(4, 6)
+        project_round(2)
+
+    def steps(*calls):
+        def run():
+            for f, i in calls:
+                f(i)
+
+        return run
+
+    attend(
+        qkv, qkv, D, hot1, o1, inv1, e1_hbm,
+        lambda i: at_head(
+            i, h0=steps((out_third, 1), (out_second, 3), (out_first, 4)), h1=second_round,
+            h2=steps((out_first, 5), (out_first, turned)), h4=third_round, h5=steps((out_third, 3), (out_second, 4)),
+        ),
+    )
     out_ready(3)
-    out_third(4)
-    out_second(5)
     unpack_pairs(6, 12)
 
     def second_norm(t):
@@ -687,22 +717,20 @@
         n2t[:, rows] = (unit * vector(2) + vector(3)).astype(BF).T
         n3t[:, rows] = (unit * vector(4) + vector(5)).astype(BF).T
 
-    loop(0, 4, second_norm)
+    loop(0, TILES, second_norm)
     project(wkv, n3t, kv)
     send_kv = remote(kv, far, ks.at[0], kr.at[0], branch=1 - b)
     send_kv.start()
     project(wquery, n2t, cq)
-
-    def last_weights(i):
-        @pl.when(i == 2)
-        def _():
-            out_ready(4)
-            out_third(5)
-
     send_kv.wait_recv()
-    attend(cq, far, 0, hot2, o2, inv2, e2_hbm, last_weights)
+    attend(
+        cq, far, 0, hot2, o2, inv2, e2_hbm,
+        lambda i: at_head(i, h1=steps((out_third, 4), (out_second, 5)), h5=steps((out_third, 5))),
+    )
+    out_ready(4)
     unpack_pairs(12, 18)
     out_ready(5)
+    out_ready(turned)
     for c in range(3):
         wdown[:, pl.ds(128 * c, 128)] = net[:, :, pl.ds(DOWN + 96 * c, 96), :].reshape(1536, 128)
     for i in range(len(OUT_PIECES)):
@@ -757,8 +785,8 @@
         dot[:, rows] = mm_nt(wcross[...], dcross16).astype(BF)
 
     cot_copy.wait()
-    loop(0, 4, feed_forward)
-    for i in (2, 3):
+    loop(0, TILES, feed_forward)
+    for i in (TILES - 2, TILES - 1):
         out_copy(i).wait()
 
     def down_grad(i):
@@ -811,7 +839,7 @@
     put_pair(LEAD + 24 * 20, g_kv[:, 640:], g_cross[:, :128])
     back_first(2)
     back_second(1)
-    loop(0, 4, third_back)
+    loop(0, TILES, third_back)
     gself[...] = mm(o1[...].astype(BF), dcr[...])
     back_ready(0)
 
@@ -895,7 +923,7 @@
         stage32[t % 2] = dh[rows, :] + normalise_back(unit, scale, dn1 * vector(0))
         gin_copy(t).start()
 
-    loop(0, 4, first_back)
+    loop(0, TILES, first_back)
     blocks = [vg0[r : r + 1, 128 * c : 128 * c + 128] for r in range(2) for c in range(3)]
     late[pl.ds(j, 1)] = jnp.concatenate(blocks + [jnp.zeros((2, 128), F32)], 0)[None]
 
@@ -948,11 +976,11 @@
         far_square(k).wait_send()
     send_kv.wait_send()
     send_dkv.wait_send()
-    for i in (2, 3):
+    for i in (TILES - 2, TILES - 1):
         gin_copy(i).wait()
 
 
-def step(x, cot, pflat, seg):
+def step(x, cot, params, seg):
     dma = pltpu.SemaphoreType.DMA
     v = pltpu.VMEM
     whole = pl.BlockSpec(memory_space=v)
@@ -965,7 +993,7 @@
             shape((N, D), BF), shape((N, D), F32), shape((FLAT, 128), F32), shape((1, 128), F32),
             shape((HEADS, N, N), BF), shape((HEADS, N, N), BF),
         ),
-        in_specs=[hbm, hbm, whole, whole],
+        in_specs=[hbm, hbm, hbm, whole],
         out_specs=(hbm, hbm, whole, whole, hbm, hbm),
         scratch_shapes=[
             v((4, 4, ROWS, 128), BF), v((3, 4, ROWS, 128), BF), v((3, ROWS, 128), BF), v((3, ROWS, 128), BF),
@@ -979,16 +1007,17 @@
             v((D, N), BF), v((2 * D, N), BF), v((2 * D, N), BF), v((D, D), F32),
             v((2, N, N), BF), v((2, N, 128), BF), v((2, N, N // 2), F32), v((HEADS, N), F32), v((HEADS, N), F32), v((32, N), BF), v((32, N), BF), v((32, N), BF),
             v((2, TILE, D), BF), v((2, TILE, D), F32), v((N, D), BF), v((N, D), BF), v((8, 128), F32),
+            v(params.shape, F32),
             dma((n_out, 3)), dma((n_out, 3)), dma((n_out, 3)), dma((n_out, 3)), dma((n_out, 2)), dma((n_out, 2)),
             dma((n_back, 4)), dma((n_back, 4)), dma((n_back, 3)), dma((n_back, 3)), dma((n_back, 2)), dma((n_back, 2)),
             dma((2,)), dma((2,)), dma((2, 3)), dma((2, 3)), dma((15,)), dma((15,)), dma((31,)), dma((31,)),
-            dma((2,)), dma((2,)), dma((2,)), dma((2,)),
+            dma((2,)), dma((2,)), dma((2,)), dma((5,)),
         ],
         compiler_params=pltpu.CompilerParams(
             collective_id=0, has_side_effects=True, vmem_limit_bytes=63 * 1024 * 1024
         ),
         name="step",
-    )(x, cot, pflat, seg)
+    )(x, cot, params, seg)
 
 
 def finish_kernel(threshold, flat, square, params, first, second, out, grad_in, *rest):
@@ -1095,8 +1124,7 @@
 def fast_device(frames_in, seg_ids, cotangent, params, first_moment, second_moment):
     count = lax.axis_size("frames")
     size = params.shape[1]
-    pflat = jnp.pad(params, ((0, 0), (0, FLAT * 128 - size))).reshape(FLAT, 128)
-    result, input_grad, flat, square, _, _ = step(frames_in[0], cotangent[0], pflat, seg_ids)
+    result, input_grad, flat, square, _, _ = step(frames_in[0], cotangent[0], params, seg_ids)
     total_params = size * count
     total_rows = frames_in.shape[1] * count
     threshold = 0.01 * math.sqrt(2.0 * total_params * total_rows)

time: 160 us -> 151 us (0.944)
  Pallas kernels: 156 us -> 150 us
  local copies, waits for them, and re-layouts: 2.48 us -> 0 us
    pallas_call x1, Pallas kernels: 151 us -> 144 us  [step(): pl.pallas_call(step_kernel, out_shape=(shape((N, D), BF), shape((N, D), F...]
    pad x1 -> x0, local copies, waits for them, and re-layouts: 2.48 us -> none  [fast_device(): pflat = jnp.pad(params, ((0, 0), (0, FLAT * 128 - size))).reshape(FLAT, 128)]
where the time goes in v4:
time: 151 us
  Pallas kernels  150 us (99%)
    pallas_call x1, Pallas kernels, step(): pl.pallas_call(step_kernel, out_shape=(shape((N, D), BF), shape((N, D), F...  144 us
    pallas_call x1, Pallas kernels, finish(): pl.pallas_call(partial(finish_kernel, threshold), out_shape=(like, shape(...  5.64 us

profile of v4, /device:TPU:0, one launch (start us, length us, event | category | flops | bytes accessed | tf_op | source)
XLA Modules:
  0.0 150.9 jit_solution(9360143757820733375)
XLA Ops:
  0.6 144.5 %step.1 = (bf16[1024,384]{1,0:T(8,128)(2,1)}, f32[1024,384]{1,0:T(8,128)}, f32[1160,128]{1,0:T(8,128)}, f32[1,128]{1,0:T(1,128)}, bf16[8,1024,1024]{2,1,0:T(8,128)(2,1)}, /*index=5*/bf16[8,1024,1024]{2,1,0:T(8,128)(2,1)}) custom-call(bf16[1024,384]{1,0:T(8,128)(2,1)} %bitcast.5, bf16[1024,384]{1,0:T(8,128)(2,1)} %bitcast.6, f32[1,147720]{1,0:T(1,128)} %params.1, ...), custom_call_target="tpu_custom_call" | custom-call | tf_op jit(solution)/shard_map/step/pallas_call | solution.py:990
  145.1 5.6 %finish.1 = (f32[1,147720]{1,0:T(1,128)}, f32[1,264]{1,0:T(1,128)}, f32[1,1]{1,0:T(1,128)}, f32[1,147720]{1,0:T(1,128)}, f32[1,147720]{1,0:T(1,128)}, /*index=5*...) custom-call(f32[1160,128]{1,0:T(8,128)} %get-tuple-element.20.flat, f32[1,128]{1,0:T(1,128)} %get-tuple-element.21.square, ...), custom_call_target="tpu_custom_call" | custom-call | tf_op jit(solution)/shard_map/finish/pallas_call | solution.py:1109

commit v5 on v4

--- a/solution.py
+++ b/solution.py
@@ -319,8 +319,9 @@
     (net, r1, s2, r2, vec, vflat, vg, vg0, vsum, vr1, vr2, late, nb) = (next(it) for _ in range(13))
     (wqkv, wself, wquery, wkv, wcross, wup, wdown) = (next(it) for _ in range(7))
     (at, qkv, o1, h, n2t, n3t, cq, kv, far, o2) = (next(it) for _ in range(10))
-    (n4t, zt, du, dffn, dh, dcr, dot, dkv, dkv_far, gself) = (next(it) for _ in range(10))
-    (ring, keys, scores, inv1, inv2, hot1, hot2, mask, stage16, stage32, x, cot, sq, praw) = (next(it) for _ in range(14))
+    (n4t, zt, du, dffn, dh, dcr, dot, dkv_far, gself) = (next(it) for _ in range(9))
+    dkv = kv
+    (ring, keys, scores, inv1, inv2, hot1, hot2, mask, stage16, x, cot, sq, praw) = (next(it) for _ in range(13))
     (as1, ar1, as2, ar2, as3, ar3, bs1, br1, bs2, br2, bs3, br3, ks, kr, vs, vr, ls, lr, ns, nr, es, os, gs, xs) = (
         next(it) for _ in range(24)
     )
@@ -733,6 +734,7 @@
     out_ready(turned)
     for c in range(3):
         wdown[:, pl.ds(128 * c, 128)] = net[:, :, pl.ds(DOWN + 96 * c, 96), :].reshape(1536, 128)
+    send_kv.wait_send()
     for i in range(len(OUT_PIECES)):
         for k in others:
             a1(i, k).wait_send()
@@ -756,8 +758,8 @@
         dffn[rows, :] = dffn16
         ffn_out = jnp.zeros((TILE, D), F32)
         dn4 = jnp.zeros((TILE, D), F32)
-        for c in range(4):
-            part = slice(c * D, (c + 1) * D)
+        for c in range(FF // 512):
+            part = slice(c * 512, (c + 1) * 512)
             u = mm(n4, wup[:, part])
             share = 0.5 * (1.0 + lax.erf(u * math.sqrt(0.5)))
             slope = share + u * (jnp.exp(-0.5 * u * u) * (1.0 / math.sqrt(2.0 * math.pi)))
@@ -853,9 +855,10 @@
         v1(k).start()
 
     def round_grad(i):
-        g = [mm_nt(at[...], qkv[pl.ds(D * m + 128 * i, 128), :]) for m in range(3)]
-        put_pair(LEAD + 96 * i, g[0], g[1])
-        put_pair(LEAD + 96 * i + 48, g[2], gself[:, 128 * i : 128 * i + 128])
+        parts = [qkv[pl.ds(D * m + 128 * i, 128), :] for m in range(3)]
+        g = mm_nt(at[...], jnp.concatenate(parts, 0))
+        put_pair(LEAD + 96 * i, g[:, :128], g[:, 128:256])
+        put_pair(LEAD + 96 * i + 48, g[:, 256:], gself[:, 128 * i : 128 * i + 128])
         back_first(3 + i)
 
     def vectors_on():
@@ -907,7 +910,7 @@
     back_second(4)
 
     def gin_copy(t):
-        return pltpu.make_async_copy(stage32.at[t % 2], gin_hbm.at[rows_at(t, TILE)], gs.at[t % 2])
+        return pltpu.make_async_copy(dh.at[rows_at(t, TILE)], gin_hbm.at[rows_at(t, TILE)], gs.at[t])
 
     def first_back(t):
         rows = rows_at(t, TILE)
@@ -915,12 +918,7 @@
         unit, scale = normalise(x[rows, :].astype(F32))
         vg0[0:1, :] += jnp.sum(dn1 * unit, 0, keepdims=True)
         vg0[1:2, :] += jnp.sum(dn1, 0, keepdims=True)
-
-        @pl.when(t >= 2)
-        def _():
-            gin_copy(t - 2).wait()
-
-        stage32[t % 2] = dh[rows, :] + normalise_back(unit, scale, dn1 * vector(0))
+        dh[rows, :] = dh[rows, :] + normalise_back(unit, scale, dn1 * vector(0))
         gin_copy(t).start()
 
     loop(0, TILES, first_back)
@@ -974,9 +972,8 @@
         far_vector(k).wait_send()
     for k in range(1, 32):
         far_square(k).wait_send()
-    send_kv.wait_send()
     send_dkv.wait_send()
-    for i in (TILES - 2, TILES - 1):
+    for i in range(TILES):
         gin_copy(i).wait()
 
 
@@ -1004,9 +1001,9 @@
             v((D, N), BF), v((3 * D, N), BF), v((D, N), F32), v((N, D), F32), v((D, N), BF), v((D, N), BF),
             v((D, N), BF), v((2 * D, N), BF), v((2 * D, N), BF), v((D, N), F32),
             v((D, N), BF), v((FF, N), BF), v((N, FF), BF), v((N, D), BF), v((N, D), F32), v((N, D), BF),
-            v((D, N), BF), v((2 * D, N), BF), v((2 * D, N), BF), v((D, D), F32),
+            v((D, N), BF), v((2 * D, N), BF), v((D, D), F32),
             v((2, N, N), BF), v((2, N, 128), BF), v((2, N, N // 2), F32), v((HEADS, N), F32), v((HEADS, N), F32), v((32, N), BF), v((32, N), BF), v((32, N), BF),
-            v((2, TILE, D), BF), v((2, TILE, D), F32), v((N, D), BF), v((N, D), BF), v((8, 128), F32),
+            v((2, TILE, D), BF), v((N, D), BF), v((N, D), BF), v((8, 128), F32),
             v(params.shape, F32),
             dma((n_out, 3)), dma((n_out, 3)), dma((n_out, 3)), dma((n_out, 3)), dma((n_out, 2)), dma((n_out, 2)),
             dma((n_back, 4)), dma((n_back, 4)), dma((n_back, 3)), dma((n_back, 3)), dma((n_back, 2)), dma((n_back, 2)),
@@ -1036,17 +1033,15 @@
                 pltpu.make_async_copy(src.at[at], by.at[at], way_in.at[i, k]),
                 pltpu.make_async_copy(by.at[at], dst.at[at], way_out.at[i, k]),
             ))
-    for come, _ in moves:
-        come.start()
     reads = []
     for i in range(parts):
         at = pl.ds(i * rows * 128, rows * 128)
+        here = pl.ds(i * rows, rows)
         for k, (src, dst) in enumerate(((params, p), (first, m), (second, v))):
-            c = pltpu.make_async_copy(
-                src.at[:, at].reshape(rows, 128), dst.at[pl.ds(i * rows, rows)], big_in.at[i, k]
-            )
+            c = pltpu.make_async_copy(src.at[:, at].reshape(rows, 128), dst.at[here], big_in.at[i, k])
             c.start()
             reads.append(c)
+        moves[i][0].start()
     for k, (src, dst) in enumerate(((params, tail_p), (first, tail_m), (second, tail_v))):
         c = pltpu.make_async_copy(src.at[:, pl.ds(main, size - main)], dst, tail_in.at[k])
         c.start()
@@ -1069,10 +1064,6 @@
 
     writes = []
     for i in range(parts):
-        come, go = moves[i]
-        come.wait()
-        go.start()
-        writes.append(go)
         for c in reads[3 * i : 3 * i + 3]:
             c.wait()
         here = pl.ds(i * rows, rows)
@@ -1084,6 +1075,10 @@
             )
             c.start()
             writes.append(c)
+        come, go = moves[i]
+        come.wait()
+        go.start()
+        writes.append(go)
     for c in reads[3 * parts :]:
         c.wait()
     wide = jnp.concatenate([flat[main // 128 + i : main // 128 + i + 1] for i in range(3)], 1)

time: 151 us -> 150 us (level)
  no operation moved by 1% of the time
where the time goes in v5:
time: 150 us; the launch traced here: 149 us
  Pallas kernels  149 us (99%)
    pallas_call x1, Pallas kernels, step(): pl.pallas_call(step_kernel, out_shape=(shape((N, D), BF), shape((N, D), F...  143 us
    pallas_call x1, Pallas kernels, finish(): pl.pallas_call(partial(finish_kernel, threshold), out_shape=(like, shape(...  5.6 us

profile of v5, /device:TPU:0, one launch (start us, length us, event | category | flops | bytes accessed | tf_op | source)
XLA Modules:
  0.0 149.4 jit_solution(10082702844350390909)
XLA Ops:
  0.6 143.0 %step.1 = (bf16[1024,384]{1,0:T(8,128)(2,1)}, f32[1024,384]{1,0:T(8,128)}, f32[1160,128]{1,0:T(8,128)}, f32[1,128]{1,0:T(1,128)}, bf16[8,1024,1024]{2,1,0:T(8,128)(2,1)}, /*index=5*/bf16[8,1024,1024]{2,1,0:T(8,128)(2,1)}) custom-call(bf16[1024,384]{1,0:T(8,128)(2,1)} %bitcast.5, bf16[1024,384]{1,0:T(8,128)(2,1)} %bitcast.6, f32[1,147720]{1,0:T(1,128)} %params.1, ...), custom_call_target="tpu_custom_call" | custom-call | tf_op jit(solution)/shard_map/step/pallas_call | solution.py:987
  143.6 5.6 %finish.1 = (f32[1,147720]{1,0:T(1,128)}, f32[1,264]{1,0:T(1,128)}, f32[1,1]{1,0:T(1,128)}, f32[1,147720]{1,0:T(1,128)}, f32[1,147720]{1,0:T(1,128)}, /*index=5*...) custom-call(f32[1160,128]{1,0:T(8,128)} %get-tuple-element.20.flat, f32[1,128]{1,0:T(1,128)} %get-tuple-element.21.square, ...), custom_call_target="tpu_custom_call" | custom-call | tf_op jit(solution)/shard_map/finish/pallas_call | solution.py:1104

commit v6 on v5

--- a/solution.py
+++ b/solution.py
@@ -541,7 +541,7 @@
     out_second(2)
     out_ready(0)
 
-    vflat[...] = jnp.zeros((48, 128), F32)
+    vflat[...] = jnp.zeros((56, 128), F32)
     lane = lax.broadcasted_iota(jnp.int32, (8, 128), 1)
     sub = lax.broadcasted_iota(jnp.int32, (8, 128), 0)
     for i in range(16):
@@ -994,7 +994,7 @@
         out_specs=(hbm, hbm, whole, whole, hbm, hbm),
         scratch_shapes=[
             v((4, 4, ROWS, 128), BF), v((3, 4, ROWS, 128), BF), v((3, ROWS, 128), BF), v((3, ROWS, 128), BF),
-            v((16, D), F32), v((48, 128), F32), v((16, D), F32), v((8, D), F32), v((16, D), F32), v((3, 16, D), F32),
+            v((16, D), F32), v((56, 128), F32), v((16, D), F32), v((8, D), F32), v((16, D), F32), v((3, 16, D), F32),
             v((3, 16, D), F32), v((16, 8, 128), F32), v((32, 8, 128), F32),
             v((3 * D, D), BF), v((D, D), BF), v((D, D), BF), v((2 * D, D), BF), v((D, D), BF), v((D, FF), BF),
             v((FF, D), BF),

time: 150 us -> 150 us (level)
  no operation moved by 1% of the time
where the time goes in v6:
time: 150 us
  Pallas kernels  149 us (99%)
    pallas_call x1, Pallas kernels, step(): pl.pallas_call(step_kernel, out_shape=(shape((N, D), BF), shape((N, D), F...  144 us
    pallas_call x1, Pallas kernels, finish(): pl.pallas_call(partial(finish_kernel, threshold), out_shape=(like, shape(...  5.6 us

profile of v6, /device:TPU:0, one launch (start us, length us, event | category | flops | bytes accessed | tf_op | source)
XLA Modules:
  0.0 150.1 jit_solution(1129693240565310278)
XLA Ops:
  0.6 143.7 %step.1 = (bf16[1024,384]{1,0:T(8,128)(2,1)}, f32[1024,384]{1,0:T(8,128)}, f32[1160,128]{1,0:T(8,128)}, f32[1,128]{1,0:T(1,128)}, bf16[8,1024,1024]{2,1,0:T(8,128)(2,1)}, /*index=5*/bf16[8,1024,1024]{2,1,0:T(8,128)(2,1)}) custom-call(bf16[1024,384]{1,0:T(8,128)(2,1)} %bitcast.5, bf16[1024,384]{1,0:T(8,128)(2,1)} %bitcast.6, f32[1,147720]{1,0:T(1,128)} %params.1, ...), custom_call_target="tpu_custom_call" | custom-call | tf_op jit(solution)/shard_map/step/pallas_call | solution.py:987
  144.3 5.6 %finish.1 = (f32[1,147720]{1,0:T(1,128)}, f32[1,264]{1,0:T(1,128)}, f32[1,1]{1,0:T(1,128)}, f32[1,147720]{1,0:T(1,128)}, f32[1,147720]{1,0:T(1,128)}, /*index=5*...) custom-call(f32[1160,128]{1,0:T(8,128)} %get-tuple-element.20.flat, f32[1,128]{1,0:T(1,128)} %get-tuple-element.21.square, ...), custom_call_target="tpu_custom_call" | custom-call | tf_op jit(solution)/shard_map/finish/pallas_call | solution.py:1104
